TPU v7x, 32 devices: a whole 2x2x4 slice. The times are simulated.
32 devices in a mesh: dp: 2 (over x), fsdp: 8 (over z, y), seq: 2 (over core).
Axes of the slice: x: 2, y: 2, z: 4, core: 2. Of those that a mesh axis runs over, the one named last changes fastest.
Arguments:
- tokens_in: bfloat16 [16, 1040, 1024], P(('dp', 'fsdp'), 'seq'), may hold values from -6 to 6
- key_mask: int32 [16, 1040], P(('dp', 'fsdp')), may hold values from 0 to 1, as said below
- attn_weights: bfloat16 [2, 1024, 4096], P(None, 'fsdp')
- mlp_weights: bfloat16 [2, 1024, 8192], P(None, 'fsdp')
- vectors: bfloat16 [2, 14, 1024], P(None, None, 'fsdp')
- cotangent: bfloat16 [16, 1040, 1024], P(('dp', 'fsdp'), 'seq'), may hold values from -6 to 6
- first_attn: float32 [2, 1024, 4096], P(None, 'fsdp'), may hold values from -40 to 40
- second_attn: float32 [2, 1024, 4096], P(None, 'fsdp'), may hold values from 0.832 to 8.32
- first_mlp: float32 [2, 1024, 8192], P(None, 'fsdp'), may hold values from -40 to 40
- second_mlp: float32 [2, 1024, 8192], P(None, 'fsdp'), may hold values from 0.832 to 8.32
- first_vec: float32 [2, 14, 1024], P(None, None, 'fsdp'), may hold values from -80 to 80
- second_vec: float32 [2, 14, 1024], P(None, None, 'fsdp'), may hold values from 3.328 to 33.28
Outputs:
- tokens_out: float32 [16, 1040, 1024], P(('dp', 'fsdp'), 'seq')
- grad_tokens: float32 [16, 1040, 1024], P(('dp', 'fsdp'), 'seq')
- grad_attn: float32 [2, 1024, 4096], P(None, 'fsdp')
- grad_mlp: float32 [2, 1024, 8192], P(None, 'fsdp')
- grad_vectors: float32 [2, 14, 1024], P(None, None, 'fsdp')
- step_attn: float32 [2, 1024, 4096], P(None, 'fsdp')
- step_mlp: float32 [2, 1024, 8192], P(None, 'fsdp')
- step_vectors: float32 [2, 14, 1024], P(None, None, 'fsdp')
- new_first_attn: float32 [2, 1024, 4096], P(None, 'fsdp')
- new_second_attn: float32 [2, 1024, 4096], P(None, 'fsdp')
- new_first_mlp: float32 [2, 1024, 8192], P(None, 'fsdp')
- new_second_mlp: float32 [2, 1024, 8192], P(None, 'fsdp')
- new_first_vec: float32 [2, 14, 1024], P(None, None, 'fsdp')
- new_second_vec: float32 [2, 14, 1024], P(None, None, 'fsdp')
Inputs may be any that keep to these rules, and one draw needn't show every extreme that they name: `key_mask`: each image's row is 1 on its first slots and 0 on the rest; at least 910 ones and at least one 0 in every row.
All inputs are finite; a program needn't handle non-finite values.
Results may differ from a plain program's by a relative error of at most 0.023.
Values may be sent and summed in bfloat16 or wider, within the bound.
No kernel may reach another device: no remote copies, remote signals or barrier semaphores. Data moves between devices by JAX's collectives and lax.ppermute only.
A program may use at most 320 MiB of HBM per device.

v0:
```python
import jax
import jax.numpy as jnp
from jax import lax
from jax.sharding import PartitionSpec as P

HD = 64


norm_eps = 1e-06
neg_large = -1e30
beta_first = 0.9
beta_second = 0.999
adam_eps = 1e-08
decay_rate = 0.05
rate_matrix = 0.01
rate_vector = 0.05
step_count = 10.0


def layer_norm(values, norm_gain, norm_shift):
    center = values - jnp.mean(values, axis=-1, keepdims=True)
    spread = jnp.mean(center * center, axis=-1, keepdims=True)
    return center * lax.rsqrt(spread + norm_eps) * norm_gain + norm_shift


def gelu_exact(values):
    return jax.nn.gelu(values, approximate=False)


def contract_last(left_side, right_side):
    return lax.dot_general(
        left_side,
        right_side,
        (((left_side.ndim - 1,), (1,)), ((), ())),
        preferred_element_type=jnp.float32,
    )


def contract_rows(left_side, right_side):
    return lax.dot_general(
        left_side, right_side, (((0, 1), (0, 1)), ((), ())), preferred_element_type=jnp.float32
    )


def masked_scores(query_rows, key_rows, valid_keys):
    scores = contract_last(query_rows, key_rows) * query_rows.shape[-1] ** (-0.5)
    return jnp.where(valid_keys[None, :] > 0, scores, neg_large)


def attend_item(item_set):
    query_rows, key_rows, value_rows, valid_keys = item_set
    scores = masked_scores(query_rows, key_rows, valid_keys)
    row_top = jnp.max(scores, axis=-1, keepdims=True)
    exp_terms = jnp.exp(scores - row_top)
    row_total = jnp.sum(exp_terms, axis=-1, keepdims=True)
    attention = (exp_terms / row_total).astype(jnp.bfloat16)
    mixed_rows = jnp.dot(attention, value_rows, preferred_element_type=jnp.float32)
    return (mixed_rows.astype(jnp.bfloat16), row_top[:, 0] + jnp.log(row_total[:, 0]))


def attend_back(item_set):
    query_rows, key_rows, value_rows, valid_keys, log_total, grad_rows = item_set
    score_scale = query_rows.shape[-1] ** (-0.5)
    scores = masked_scores(query_rows, key_rows, valid_keys)
    attention = jnp.exp(scores - log_total[:, None])
    grad_value = lax.dot_general(
        attention.astype(jnp.bfloat16),
        grad_rows,
        (((0,), (0,)), ((), ())),
        preferred_element_type=jnp.float32,
    )
    grad_attention = contract_last(grad_rows, value_rows)
    inner_sum = jnp.sum(attention * grad_attention, axis=-1, keepdims=True)
    grad_scores = (attention * (grad_attention - inner_sum)).astype(jnp.bfloat16)
    grad_query = jnp.dot(grad_scores, key_rows, preferred_element_type=jnp.float32) * score_scale
    grad_key = (
        lax.dot_general(
            grad_scores, query_rows, (((0,), (0,)), ((), ())), preferred_element_type=jnp.float32
        )
        * score_scale
    )
    return jnp.stack([grad_query, grad_key, grad_value]).astype(jnp.bfloat16)


def forward_layer(inputs, mask_heads, attn_full, mlp_full, vectors_full):
    model_width = attn_full.shape[0]
    hidden = mlp_full.shape[1] // 2
    vec_rows = vectors_full.astype(jnp.float32)
    n_seq = lax.axis_size("seq")
    images, token_rows, _ = inputs.shape
    length = token_rows * n_seq
    group_width = model_width // n_seq
    per_group = group_width // HD
    normed = layer_norm(inputs, vec_rows[0], vec_rows[1]).astype(jnp.bfloat16)
    bias_qkv = jnp.concatenate([vec_rows[2], jnp.zeros_like(vec_rows[2]), vec_rows[3]])
    qkv = (
        jnp.dot(normed, attn_full[:, : 3 * model_width], preferred_element_type=jnp.float32)
        + bias_qkv
    ).astype(jnp.bfloat16)
    heads = lax.all_to_all(
        qkv.reshape(images, token_rows, 3, n_seq, group_width),
        "seq",
        split_axis=3,
        concat_axis=1,
        tiled=True,
    )
    stacked = (
        heads.reshape(images, length, 3, per_group, HD)
        .transpose(2, 0, 3, 1, 4)
        .reshape(3, images * per_group, length, HD)
    )
    mixed_items, log_total = lax.map(attend_item, (stacked[0], stacked[1], stacked[2], mask_heads))
    mixed_heads = (
        mixed_items.reshape(images, per_group, length, HD)
        .transpose(0, 2, 1, 3)
        .reshape(images, length, 1, group_width)
    )
    mixed_rows = lax.all_to_all(
        mixed_heads, "seq", split_axis=1, concat_axis=2, tiled=True
    ).reshape(images, token_rows, model_width)
    branch = contract_last(mixed_rows, attn_full[:, 3 * model_width :]) + vec_rows[4]
    middle = inputs + vec_rows[5] * branch
    normed_two = layer_norm(middle, vec_rows[6], vec_rows[7]).astype(jnp.bfloat16)
    pre_act = jnp.dot(
        normed_two, mlp_full[:, :hidden], preferred_element_type=jnp.float32
    ) + vec_rows[10:].reshape(hidden)
    active = gelu_exact(pre_act).astype(jnp.bfloat16)
    mlp_out = contract_last(active, mlp_full[:, hidden:]) + vec_rows[8]
    output = middle + vec_rows[9] * mlp_out
    saved_set = (
        inputs,
        normed,
        stacked,
        log_total,
        mixed_rows,
        branch,
        middle,
        normed_two,
        pre_act,
        active,
        mlp_out,
    )
    return (output, saved_set)


def backward_layer(upstream, saved_set, attn_full, mlp_full, vectors_full, mask_heads):
    (
        inputs,
        normed,
        stacked,
        log_total,
        mixed_rows,
        branch,
        middle,
        normed_two,
        pre_act,
        active,
        mlp_out,
    ) = saved_set
    model_width = attn_full.shape[0]
    hidden = mlp_full.shape[1] // 2
    vec_rows = vectors_full.astype(jnp.float32)
    n_seq = lax.axis_size("seq")
    images, token_rows, _ = upstream.shape
    length = token_rows * n_seq
    group_width = model_width // n_seq
    per_group = group_width // HD
    grad_scale_two = jnp.sum(upstream * mlp_out, axis=(0, 1))
    grad_mlp_out = (upstream * vec_rows[9]).astype(jnp.bfloat16)
    grad_bias_down = jnp.sum(grad_mlp_out.astype(jnp.float32), axis=(0, 1))
    grad_down = contract_rows(grad_mlp_out, active)
    grad_active = jnp.dot(grad_mlp_out, mlp_full[:, hidden:], preferred_element_type=jnp.float32)
    _, gelu_pull = jax.vjp(gelu_exact, pre_act)
    grad_pre = gelu_pull(grad_active)[0].astype(jnp.bfloat16)
    grad_bias_up = jnp.sum(grad_pre.astype(jnp.float32), axis=(0, 1))
    grad_up = contract_rows(normed_two, grad_pre)
    grad_normed_two = contract_last(grad_pre, mlp_full[:, :hidden])
    _, second_pull = jax.vjp(layer_norm, middle, vec_rows[6], vec_rows[7])
    grad_mid_norm, grad_gain_two, grad_shift_two = second_pull(grad_normed_two)
    grad_middle = upstream + grad_mid_norm
    grad_scale_one = jnp.sum(grad_middle * branch, axis=(0, 1))
    grad_branch = (grad_middle * vec_rows[5]).astype(jnp.bfloat16)
    grad_bias_proj = jnp.sum(grad_branch.astype(jnp.float32), axis=(0, 1))
    grad_proj = contract_rows(grad_branch, mixed_rows)
    grad_mixed = jnp.dot(
        grad_branch, attn_full[:, 3 * model_width :], preferred_element_type=jnp.float32
    ).astype(jnp.bfloat16)
    grad_heads = lax.all_to_all(
        grad_mixed.reshape(images, token_rows, n_seq, group_width),
        "seq",
        split_axis=2,
        concat_axis=1,
        tiled=True,
    )
    grad_items = (
        grad_heads.reshape(images, length, per_group, HD)
        .transpose(0, 2, 1, 3)
        .reshape(images * per_group, length, HD)
    )
    grad_stack = lax.map(
        attend_back, (stacked[0], stacked[1], stacked[2], mask_heads, log_total, grad_items)
    )
    grad_stack = (
        grad_stack.reshape(images, per_group, 3, length, HD)
        .transpose(0, 3, 2, 1, 4)
        .reshape(images, length, 3, 1, group_width)
    )
    grad_qkv = lax.all_to_all(grad_stack, "seq", split_axis=1, concat_axis=3, tiled=True).reshape(
        images, token_rows, 3 * model_width
    )
    grad_qkv_sum = jnp.sum(grad_qkv.astype(jnp.float32), axis=(0, 1))
    grad_qkv_weight = contract_rows(normed, grad_qkv)
    grad_normed = contract_last(grad_qkv, attn_full[:, : 3 * model_width])
    _, first_pull = jax.vjp(layer_norm, inputs, vec_rows[0], vec_rows[1])
    grad_in_norm, grad_gain_one, grad_shift_one = first_pull(grad_normed)
    grad_inputs = grad_middle + grad_in_norm
    grad_attn = jnp.concatenate([grad_qkv_weight, grad_proj], axis=1)
    grad_mlp = jnp.concatenate([grad_up, grad_down], axis=1)
    grad_rows = jnp.stack(
        [
            grad_gain_one,
            grad_shift_one,
            grad_qkv_sum[:model_width],
            grad_qkv_sum[2 * model_width :],
            grad_bias_proj,
            grad_scale_one,
            grad_gain_two,
            grad_shift_two,
            grad_bias_down,
            grad_scale_two,
        ]
    )
    grad_vec = jnp.concatenate(
        [grad_rows, grad_bias_up.reshape(hidden // model_width, model_width)], axis=0
    )
    return (grad_inputs, (grad_attn, grad_mlp, grad_vec))


def adam_step(weights, gradient, moment_one, moment_two, step_rate, decay_weight):
    one_new = beta_first * moment_one + (1.0 - beta_first) * gradient
    two_new = beta_second * moment_two + (1.0 - beta_second) * gradient * gradient
    one_hat = one_new / (1.0 - beta_first**step_count)
    two_hat = two_new / (1.0 - beta_second**step_count)
    change = -step_rate * (
        one_hat / (jnp.sqrt(two_hat) + adam_eps) + decay_weight * weights.astype(jnp.float32)
    )
    return (change, one_new, two_new)


def local(
    tokens_in,
    key_mask,
    attn_weights,
    mlp_weights,
    vectors,
    cotangent,
    first_attn,
    second_attn,
    first_mlp,
    second_mlp,
    first_vec,
    second_vec,
):
    layers = attn_weights.shape[0]
    n_seq = lax.axis_size("seq")
    per_group = attn_weights.shape[2] // 4 // n_seq // HD
    mask_heads = jnp.repeat(key_mask, per_group, axis=0)
    residual = tokens_in.astype(jnp.float32)
    stored = []
    gathered_sets = []
    for layer_index in range(layers):
        weight_set = (
            lax.all_gather(attn_weights[layer_index], "fsdp", axis=0, tiled=True),
            lax.all_gather(mlp_weights[layer_index], "fsdp", axis=0, tiled=True),
            lax.all_gather(vectors[layer_index], "fsdp", axis=1, tiled=True),
        )
        residual, saved_set = forward_layer(
            residual, mask_heads, weight_set[0], weight_set[1], weight_set[2]
        )
        stored.append(saved_set)
        gathered_sets.append(weight_set)
    upstream = cotangent.astype(jnp.float32)
    layer_grads = [None] * layers
    for layer_index in reversed(range(layers)):
        weight_set = (
            lax.all_gather(attn_weights[layer_index], "fsdp", axis=0, tiled=True),
            lax.all_gather(mlp_weights[layer_index], "fsdp", axis=0, tiled=True),
            lax.all_gather(vectors[layer_index], "fsdp", axis=1, tiled=True),
        )
        upstream, local_grads = backward_layer(
            upstream, stored[layer_index], weight_set[0], weight_set[1], weight_set[2], mask_heads
        )
        owned = (
            lax.psum_scatter(
                local_grads[0].astype(jnp.bfloat16), "fsdp", scatter_dimension=0, tiled=True
            ).astype(jnp.float32),
            lax.psum_scatter(
                local_grads[1].astype(jnp.bfloat16), "fsdp", scatter_dimension=0, tiled=True
            ).astype(jnp.float32),
            lax.psum_scatter(
                local_grads[2].astype(jnp.bfloat16), "fsdp", scatter_dimension=1, tiled=True
            ).astype(jnp.float32),
        )
        owned = (
            lax.psum(owned[0].astype(jnp.bfloat16), ("dp", "seq")).astype(jnp.float32),
            lax.psum(owned[1].astype(jnp.bfloat16), ("dp", "seq")).astype(jnp.float32),
            lax.psum(owned[2].astype(jnp.bfloat16), ("dp", "seq")).astype(jnp.float32),
        )
        layer_grads[layer_index] = owned
    grad_attn = jnp.stack([layer_grads[index_one][0] for index_one in range(layers)])
    grad_mlp = jnp.stack([layer_grads[index_one][1] for index_one in range(layers)])
    grad_vectors = jnp.stack([layer_grads[index_one][2] for index_one in range(layers)])
    step_attn, one_attn, two_attn = adam_step(
        attn_weights, grad_attn, first_attn, second_attn, rate_matrix, decay_rate
    )
    step_mlp, one_mlp, two_mlp = adam_step(
        mlp_weights, grad_mlp, first_mlp, second_mlp, rate_matrix, decay_rate
    )
    step_vectors, one_vec, two_vec = adam_step(
        vectors, grad_vectors, first_vec, second_vec, rate_vector, 0.0
    )
    return (
        residual,
        upstream,
        grad_attn,
        grad_mlp,
        grad_vectors,
        step_attn,
        step_mlp,
        step_vectors,
        one_attn,
        two_attn,
        one_mlp,
        two_mlp,
        one_vec,
        two_vec,
    )


def solution(mesh):
    return jax.shard_map(
        local,
        mesh=mesh,
        in_specs=(
            P(("dp", "fsdp"), "seq", None),
            P(("dp", "fsdp"), None),
            P(None, "fsdp", None),
            P(None, "fsdp", None),
            P(None, None, "fsdp"),
            P(("dp", "fsdp"), "seq", None),
            P(None, "fsdp", None),
            P(None, "fsdp", None),
            P(None, "fsdp", None),
            P(None, "fsdp", None),
            P(None, None, "fsdp"),
            P(None, None, "fsdp"),
        ),
        out_specs=(
            P(("dp", "fsdp"), "seq", None),
            P(("dp", "fsdp"), "seq", None),
            P(None, "fsdp", None),
            P(None, "fsdp", None),
            P(None, None, "fsdp"),
            P(None, "fsdp", None),
            P(None, "fsdp", None),
            P(None, None, "fsdp"),
            P(None, "fsdp", None),
            P(None, "fsdp", None),
            P(None, "fsdp", None),
            P(None, "fsdp", None),
            P(None, None, "fsdp"),
            P(None, None, "fsdp"),
        ),
        check_vma=False,
    )
```

profile of v0, /device:TPU:0, one launch (start us, length us, event | category | flops | bytes accessed | tf_op | source)
XLA Modules:
  0.0 2304.5 jit_solution(1958127319763447503)
XLA Ops:
  16.5 23.2 %all-gather = bf16[1,14,1024]{2,0,1:T(2,128)(2,1)S(1)} all-gather(bf16[1,14,128]{2,0,1:T(2,128)(2,1)S(1)} %get-tuple-element.468), channel_id=2, replica_groups=mesh['dp'=2,'fsdp'=8,'seq'=2] {'fsdp'}, dimensions={2}, use_global_device_ids=true | all-gather | bytes 32256 | tf_op jit(solution)/shard_map/all_gather | solution.py:275
  39.9 17.4 all-gather.3
  59.9 79.7 %all-gather.11.cloned.1.call-done = bf16[1,1024,4096]{2,1,0:T(8,128)(2,1)} async-done(((bf16[1,128,4096]{2,1,0:T(8,128)(2,1)}), bf16[1,1024,4096]{2,1,0:T(8,128)(2,1)}) %all-gather.11.cloned.1.call-update) | async-done | bytes 8388624 | tf_op jit(solution)/shard_map/all_gather | solution.py:273
  198.8 72.4 %while.44 = (s32[]{:T(128)}, bf16[8,1040,64]{1,2,0:T(8,128)(2,1)}, f32[8,1040]{1,0:T(8,128)S(1)}, s32[8,1040]{1,0:T(8,128)S(1)}, bf16[8,1040,64]{2,1,0:T(8,128)(...) while((s32[]{:T(128)}, bf16[8,1040,64]{1,2,0:T(8,128)(2,1)}, ...), condition=%wide.region_5.6_spmd, body=%wide.region_2.5_spmd.sunk | while | flops 285608960 | bytes 31756240 | solution.py:112
  305.0 63.0 %all-gather.13.cloned.1.call-done = bf16[1,1024,8192]{2,1,0:T(8,128)(2,1)} async-done(((bf16[1,128,8192]{2,1,0:T(8,128)(2,1)}), bf16[1,1024,8192]{2,1,0:T(8,128)(2,1)}) %all-gather.13.cloned.1.call-update) | async-done | bytes 16777232 | tf_op jit(solution)/shard_map/all_gather | solution.py:274
  368.1 27.1 %multiply_convert_fusion.3 = (bf16[520,4096]{1,0:T(8,128)(2,1)S(1)}, f32[520,4096]{1,0:T(8,128)}, f32[520,4096]{1,0:T(8,128)}) fusion(f32[4096]{0:T(1024)S(1)} %bitcast.487, bf16[1024,8192]{1,0:T(8,128)(2,1)} %bitcast.522, f32[1,520,1024]{2,1,0:T(8,128)S(1)} %get-tuple-element.424, f32[1024]{0:T(1024)S(1)} %bitcast.513, f32[1024]{0:T(1024)S(1)} %bitcast.499, ...), kind=kOutput, calls=%fused_computation.138 | convolution fusion | flops 4505313280 | bytes 31846464 | tf_op jit(solution)/shard_map/dot_general | solution.py:124
  395.3 11.5 fusion.224
  407.2 86.7 %all-gather.15.cloned.1.call-done = bf16[1,1024,4096]{2,1,0:T(8,128)(2,1)} async-done(((bf16[1,128,4096]{2,1,0:T(8,128)(2,1)}), bf16[1,1024,4096]{2,1,0:T(8,128)(2,1)}) %all-gather.15.cloned.1.call-update) | async-done | bytes 8388624 | tf_op jit(solution)/shard_map/all_gather | solution.py:273
  552.9 68.8 %while.45 = (s32[]{:T(128)}, bf16[8,1040,64]{1,2,0:T(8,128)(2,1)S(1)}, f32[8,1040]{1,0:T(8,128)S(1)}, s32[8,1040]{1,0:T(8,128)S(1)}, bf16[8,1040,64]{2,1,0:T(8,1...) while((s32[]{:T(128)}, ...), condition=%wide.region_13.14_spmd, body=%wide.region_10.13_spmd.sunk | while | flops 285608960 | bytes 31763296 | solution.py:112
  654.4 67.8 %all-gather.17.cloned.1.call-done = bf16[1,1024,8192]{2,1,0:T(8,128)(2,1)} async-done(((bf16[1,128,8192]{2,1,0:T(8,128)(2,1)}), bf16[1,1024,8192]{2,1,0:T(8,128)(2,1)}) %all-gather.17.cloned.1.call-update) | async-done | bytes 16777232 | tf_op jit(solution)/shard_map/all_gather | solution.py:274
  722.3 28.0 %multiply_convert_fusion.2 = (bf16[520,4096]{1,0:T(8,128)(2,1)}, f32[520,4096]{1,0:T(8,128)}, f32[520,4096]{1,0:T(8,128)}) fusion(f32[4096]{0:T(1024)S(1)} %bitcast.489, bf16[1024,8192]{1,0:T(8,128)(2,1)} %bitcast.526, f32[1,520,1024]{2,1,0:T(8,128)} %copy-done.8, f32[1024]{0:T(1024)S(1)} %bitcast.511, f32[1024]{0:T(1024)S(1)} %bitcast.495, ...), kind=kOutput, calls=%fused_computation.125 | convolution fusion | flops 4505313280 | bytes 31846464 | tf_op jit(solution)/shard_map/dot_general | solution.py:124
  750.4 14.5 fusion.234
  792.1 99.1 %while.46 = (s32[]{:T(128)}, bf16[8,3,1040,64]{2,3,1,0:T(8,128)(2,1)S(1)}, s32[8,1040]{1,0:T(8,128)}, bf16[8,1040,64]{2,1,0:T(8,128)(2,1)}, bf16[8,1040,64]{2,1,...) while((s32[]{:T(128)}, ...), condition=%wide.region_20.21_spmd, body=%wide.region_18.20_spmd.sunk | while | flops 703489280 | bytes 35388936 | solution.py:200
  937.0 14.5 fusion.152
  952.4 14.3 fusion.235
  997.4 99.1 %while.47 = (s32[]{:T(128)}, bf16[8,3,1040,64]{2,3,1,0:T(8,128)(2,1)S(1)}, s32[8,1040]{1,0:T(8,128)}, bf16[8,1040,64]{2,1,0:T(8,128)(2,1)}, bf16[8,1040,64]{2,1,...) while((s32[]{:T(128)}, ...), condition=%wide.region_27.28_spmd, body=%wide.region_25.27_spmd.sunk | while | flops 703489280 | bytes 35388936 | solution.py:200
  1237.8 56.8 %reduce-scatter.11.cloned.1.call-done = bf16[128,4096]{1,0:T(8,128)(2,1)} async-done(((bf16[1024,4096]{1,0:T(8,128)(2,1)}), bf16[128,4096]{1,0:T(8,128)(2,1)}) %reduce-scatter.11.cloned.1.call-update) | async-done | bytes 1048592 | tf_op jit(solution)/shard_map/reduce_scatter | solution.py:294
  1294.7 152.5 %reduce-scatter.13.cloned.1.call-done = bf16[128,4096]{1,0:T(8,128)(2,1)} async-done(((bf16[1024,4096]{1,0:T(8,128)(2,1)}), bf16[128,4096]{1,0:T(8,128)(2,1)}) %reduce-scatter.13.cloned.1.call-update) | async-done | bytes 1048592 | tf_op jit(solution)/shard_map/reduce_scatter | solution.py:294
  1447.2 285.6 %reduce-scatter.15.cloned.1.call-done = bf16[128,8192]{1,0:T(8,128)(2,1)} async-done(((bf16[1024,8192]{1,0:T(8,128)(2,1)}), bf16[128,8192]{1,0:T(8,128)(2,1)}) %reduce-scatter.15.cloned.1.call-update) | async-done | bytes 2097168 | tf_op jit(solution)/shard_map/reduce_scatter | solution.py:297
  1732.8 286.1 %reduce-scatter.17.cloned.1.call-done = bf16[128,8192]{1,0:T(8,128)(2,1)} async-done(((bf16[1024,8192]{1,0:T(8,128)(2,1)}), bf16[128,8192]{1,0:T(8,128)(2,1)}) %reduce-scatter.17.cloned.1.call-update) | async-done | bytes 2097168 | tf_op jit(solution)/shard_map/reduce_scatter | solution.py:297
  2022.6 60.4 %reduce-scatter.19.cloned.1.call-done = bf16[128,14]{1,0:T(8,128)(2,1)} async-done(((bf16[1024,14]{1,0:T(8,128)(2,1)}), bf16[128,14]{1,0:T(8,128)(2,1)}) %reduce-scatter.19.cloned.1.call-update) | async-done | bytes 3600
  2083.9 63.2 %reduce-scatter.21.cloned.1.call-done = bf16[128,14]{1,0:T(8,128)(2,1)} async-done(((bf16[1024,14]{1,0:T(8,128)(2,1)}), bf16[128,14]{1,0:T(8,128)(2,1)}) %reduce-scatter.21.cloned.1.call-update) | async-done | bytes 3600
  2156.2 112.7 %all-reduce.4.cloned.1.call-done = (bf16[1,128,4096]{2,1,0:T(8,128)(2,1)}, bf16[1,128,4096]{2,1,0:T(8,128)(2,1)}, bf16[1,128,8192]{2,1,0:T(8,128)(2,1)}, bf16[1,128,8192]{2,1,0:T(8,128)(2,1)}) async-done(((bf16[1,128,4096]{2,1,0:T(8,128)(2,1)}, bf16[1,128,4096]{2,1,0:T(8,128)(2,1)}, bf16[1,128,8192]{2,1,0:T(8,128)(2,1)}, bf16[1,128,8192]{2,1,0:T(8,128)(2,1)}), (bf16[1,128,4096]{2,1,0:T(8,128)(2,1)}, ...) | async-done | bytes 6291472 | tf_op jit(solution)/shard_map/psum | solution.py:305
  2268.9 19.0 add_multiply_fusion
  (720 shorter events, 803.0 us)
Async XLA Ops:
  7.2 132.3 %all-gather.11.cloned.1.call-start = ((), (), s32[]{:S(2)}) async-start(), calls=%async_computation.18 | async-start | bytes 9437184 | tf_op jit(solution)/shard_map/all_gather | solution.py:273
  10.3 357.7 %all-gather.13.cloned.1.call-start = ((), (), s32[]{:S(2)}) async-start(), calls=%async_computation.19 | async-start | bytes 18874368 | tf_op jit(solution)/shard_map/all_gather | solution.py:274
  15.1 478.8 %all-gather.15.cloned.1.call-start = ((), (), s32[]{:S(2)}) async-start(), calls=%async_computation.20 | async-start | bytes 9437184 | tf_op jit(solution)/shard_map/all_gather | solution.py:273
  15.8 706.5 %all-gather.17.cloned.1.call-start = ((), (), s32[]{:S(2)}) async-start(), calls=%async_computation.21 | async-start | bytes 18874368 | tf_op jit(solution)/shard_map/all_gather | solution.py:274
  16.4 1278.3 %reduce-scatter.11.cloned.1.call-start = ((), (), s32[]{:S(2)}) async-start(), calls=%async_computation.14 | async-start | bytes 9437184 | tf_op jit(solution)/shard_map/reduce_scatter | solution.py:294
  39.8 260.1 %copy-start.66 = (f32[1,1,1024]{2,0,1:T(1,128)}, f32[1,1,1024]{2,0,1:T(1,128)S(1)}, u32[]{:S(2)}) copy-start(f32[1,1,1024]{2,0,1:T(1,128)S(1)} %get-tuple-element.461) | copy-start | bytes 12292
  39.8 260.1 %copy-start.68 = (f32[1,1,1024]{2,0,1:T(1,128)}, f32[1,1,1024]{2,0,1:T(1,128)S(1)}, u32[]{:S(2)}) copy-start(f32[1,1,1024]{2,0,1:T(1,128)S(1)} %get-tuple-element.462) | copy-start | bytes 12292
  39.8 328.3 %copy-start.77 = (f32[1,1,1024]{2,0,1:T(1,128)}, f32[1,1,1024]{2,0,1:T(1,128)S(1)}, u32[]{:S(2)}) copy-start(f32[1,1,1024]{2,0,1:T(1,128)S(1)} %get-tuple-element.459) | copy-start | bytes 12292
  39.8 328.3 %copy-start.104 = (f32[1,1,1024]{2,0,1:T(1,128)}, f32[1,1,1024]{2,0,1:T(1,128)S(1)}, u32[]{:S(2)}) copy-start(f32[1,1,1024]{2,0,1:T(1,128)S(1)} %get-tuple-element.460) | copy-start | bytes 12292
  39.8 355.4 %copy-start.70 = (f32[1,1,1024]{2,0,1:T(1,128)}, f32[1,1,1024]{2,0,1:T(1,128)S(1)}, u32[]{:S(2)}) copy-start(f32[1,1,1024]{2,0,1:T(1,128)S(1)} %get-tuple-element.457) | copy-start | bytes 12292
  39.8 355.4 %copy-start.110 = (f32[1,1,1024]{2,0,1:T(1,128)}, f32[1,1,1024]{2,0,1:T(1,128)S(1)}, u32[]{:S(2)}) copy-start(f32[1,1,1024]{2,0,1:T(1,128)S(1)} %get-tuple-element.458) | copy-start | bytes 12292
  39.9 328.2 %copy-start.72 = (f32[1,4,1024]{2,0,1:T(1,128)}, f32[1,4,1024]{2,0,1:T(1,128)S(1)}, u32[]{:S(2)}) copy-start(f32[1,4,1024]{2,0,1:T(1,128)S(1)} %slice.263) | copy-start | bytes 49156
  406.8 240.9 %copy-start.5 = (f32[1,520,1024]{2,1,0:T(8,128)}, f32[1,520,1024]{2,1,0:T(8,128)S(1)}, u32[]{:S(2)}) copy-start(f32[1,520,1024]{2,1,0:T(8,128)S(1)} %get-tuple-element.420) | copy-start | bytes 6389764
  1147.4 299.8 %reduce-scatter.13.cloned.1.call-start = ((), (), s32[]{:S(2)}) async-start(), calls=%async_computation.15 | async-start | bytes 9437184 | tf_op jit(solution)/shard_map/reduce_scatter | solution.py:294
  1167.9 564.9 %reduce-scatter.15.cloned.1.call-start = ((), (), s32[]{:S(2)}) async-start(), calls=%async_computation.16 | async-start | bytes 18874368 | tf_op jit(solution)/shard_map/reduce_scatter | solution.py:297
  1193.3 825.6 %reduce-scatter.17.cloned.1.call-start = ((), (), s32[]{:S(2)}) async-start(), calls=%async_computation.17 | async-start | bytes 18874368 | tf_op jit(solution)/shard_map/reduce_scatter | solution.py:297
  1219.5 863.6 %reduce-scatter.19.cloned.1.call-start = ((), (), s32[]{:S(2)}) async-start(), calls=%async_computation.22 | async-start | bytes 294912
  1234.0 913.1 %reduce-scatter.21.cloned.1.call-start = ((), (), s32[]{:S(2)}) async-start(), calls=%async_computation.23 | async-start | bytes 294912
  1237.6 781.4 %copy-start.13 = (f32[520,1024]{1,0:T(8,128)S(1)}, f32[520,1024]{1,0:T(8,128)}, u32[]{:S(2)}) copy-start(f32[520,1024]{1,0:T(8,128)} %copy-done.12) | copy-start | bytes 6389764
  1237.6 781.4 %copy-start.18 = (bf16[1,520,1024]{2,1,0:T(8,128)(2,1)S(1)}, bf16[1,520,1024]{2,1,0:T(8,128)(2,1)}, u32[]{:S(2)}) copy-start(bf16[1,520,1024]{2,1,0:T(8,128)(2,1)} %param.20) | copy-start | bytes 3194884
  1237.6 1031.3 %all-reduce.4.cloned.1.call-start = ((), (), s32[]{:S(2)}) async-start(), calls=%async_computation.24 | async-start | bytes 12582912 | tf_op jit(solution)/shard_map/psum | solution.py:305
  2019.0 134.8 %copy-start.47 = (bf16[2,14,128]{2,0,1:T(2,128)(2,1)S(1)}, bf16[2,14,128]{2,0,1:T(2,128)(2,1)}, u32[]{:S(2)}) copy-start(bf16[2,14,128]{2,0,1:T(2,128)(2,1)} %param.24) | copy-start | bytes 21508
  2019.0 134.8 %copy-start.91 = (f32[2,14,128]{2,0,1:T(2,128)S(1)}, f32[2,14,128]{2,0,1:T(2,128)}, u32[]{:S(2)}) copy-start(f32[2,14,128]{2,0,1:T(2,128)} %param.30) | copy-start | bytes 43012
  2019.0 134.8 %copy-start.92 = (f32[2,14,128]{2,0,1:T(2,128)S(1)}, f32[2,14,128]{2,0,1:T(2,128)}, u32[]{:S(2)}) copy-start(f32[2,14,128]{2,0,1:T(2,128)} %param.31) | copy-start | bytes 43012
  (123 other events, 2624.3 us)
Sparse Core Ops, SparseCore 0:
  10.7 128.7 all-gather.10
  142.2 225.7 all-gather.12
  370.8 123.1 all-gather.14
  496.5 225.7 all-gather.16
  1147.5 147.1 reduce-scatter.10
  1299.2 147.9 reduce-scatter.12
  1451.0 281.8 reduce-scatter.14
  1737.1 281.7 reduce-scatter.16
  2022.8 60.2 reduce-scatter.18
  2086.8 60.2 reduce-scatter.20
  2149.7 119.1 all-reduce.3
where the time goes:
time: 2320 us; the launch traced here: 2300 us
  waiting for transfers between devices  1320 us (57%)
  matrix products  486 us (21%)
  local copies, waits for them, and re-layouts  247 us (11%)
  other arithmetic  136 us (6%)
  blocking collectives  101 us (4%)
    reduce_scatter x2, waiting for transfers between devices, local(): lax.psum_scatter(local_grads[1].astype(jnp.bfloat16), 'fsdp', scatter_dim...  572 us
    reduce_scatter x2, waiting for transfers between devices, local(): lax.psum_scatter(local_grads[0].astype(jnp.bfloat16), 'fsdp', scatter_dim...  209 us
    dot_general x56, matrix products, contract_last(): lax.dot_general(left_side, right_side, (((left_side.ndim - 1,), (1,)), ((...  176 us
    all_gather x2, waiting for transfers between devices, local(): lax.all_gather(attn_weights[layer_index], 'fsdp', axis=0, tiled=True)  166 us
    all_gather x2, waiting for transfers between devices, local(): lax.all_gather(mlp_weights[layer_index], 'fsdp', axis=0, tiled=True)  131 us
    unnamed x13, waiting for transfers between devices  125 us
    psum x1, waiting for transfers between devices, local(): lax.psum(owned[0].astype(jnp.bfloat16), ('dp', 'seq')).astype(jnp.float32)  113 us
    dot_general x8, matrix products, contract_rows(): lax.dot_general(left_side, right_side, (((0, 1), (0, 1)), ((), ())), pref...  62.7 us
  transfers between devices with their start and end apart: 11, of which 11 were waited for; matrix products, arithmetic and copies ran while one was open for 17% of the time, Pallas kernels for 0%

commit v1 on v0

v1 whole, which is shorter than its diff:
```python
import functools

import jax
import jax.numpy as jnp
from jax import lax
from jax.experimental import pallas as pl
from jax.experimental.pallas import tpu as pltpu
from jax.sharding import PartitionSpec as P

HD = 64
EPS = 1e-06
B1 = 0.9
B2 = 0.999
ADAM_EPS = 1e-08
DECAY = 0.05
RATE_M = 0.01
RATE_V = 0.05
STEPS = 10.0
ROWS = 14
IZ1, IZ0, IY, IC, IX = range(5)

f32 = jnp.float32
bf16 = jnp.bfloat16
NN = (((1,), (0,)), ((), ()))
NT = (((1,), (1,)), ((), ()))
TN = (((0,), (0,)), ((), ()))
MB = 1 << 20


def dot(a, b, dims=NN):
    return lax.dot_general(a, b, dims, preferred_element_type=f32)


def sds(shape, dtype):
    return jax.ShapeDtypeStruct(shape, dtype)


def call(body, grid, ins, outs, scratch=(), ids=None, us=2, vmem=40, aliases=None, name=None):
    n_pre = 0 if ids is None else 1
    moved = sum(a.size * a.dtype.itemsize for a, s in ins if s.block_shape is not None)
    moved += sum(
        functools.reduce(lambda p, q: p * q, sh, 1) * jnp.dtype(dt).itemsize for sh, dt, _ in outs
    )
    return pl.pallas_call(
        body,
        out_shape=[sds(sh, dt) for sh, dt, _ in outs],
        grid_spec=pltpu.PrefetchScalarGridSpec(
            num_scalar_prefetch=n_pre,
            grid=grid,
            in_specs=[s for _, s in ins],
            out_specs=[s for _, _, s in outs],
            scratch_shapes=list(scratch),
        ),
        compiler_params=pltpu.CompilerParams(vmem_limit_bytes=vmem * MB),
        cost_estimate=pl.CostEstimate(flops=1, bytes_accessed=1, transcendentals=0),
        input_output_aliases=aliases or {},
        name=name,
    )(*(() if ids is None else (ids,)), *[a for a, _ in ins])


def whole(a):
    nd = a.ndim
    return pl.BlockSpec(a.shape, lambda *_: (0,) * nd)


def row_loop(total, fn):
    step = 104 if total % 104 == 0 else 8

    def body(i, carry):
        fn(pl.ds(pl.multiple_of(i * step, 8), step))
        return carry

    lax.fori_loop(0, total // step, body, 0)


def norm_stats(v):
    center = v - jnp.mean(v, axis=-1, keepdims=True)
    rstd = lax.rsqrt(jnp.mean(center * center, axis=-1, keepdims=True) + EPS)
    return center, rstd


def col_sum(v):
    return jnp.sum(v, axis=0, keepdims=True)


def weight_ins(w, rows, nb, index):
    if isinstance(w, tuple):
        spec = pl.BlockSpec((4, rows // 8, nb), lambda k, ids: (0, 0, index(k)))
        return [(p, spec) for p in w]
    return [(w, pl.BlockSpec((rows, nb), lambda k, ids: (0, index(k))))]


def weight_scratch(w, rows, nb):
    return [pltpu.VMEM((rows, nb), bf16)] if isinstance(w, tuple) else []


def weight_ref(ids, refs, spare):
    if len(refs) == 1:
        return refs[0]
    rows = refs[0].shape[1]
    for q in range(4):
        for bit, ref in ((ids[IY], refs[0]), (1 - ids[IY], refs[1])):
            spare[pl.ds(pl.multiple_of((2 * q + bit) * rows, rows), rows), :] = ref[q]
    return spare


def nn_kernel(ids, xo, xt, *rest, n_w, epi, n_extra, n_out, flip):
    w = rest[:n_w]
    extra = rest[n_w : n_w + n_extra]
    outs = rest[n_w + n_extra : n_w + n_extra + n_out]
    xf = rest[n_w + n_extra + n_out]
    half = xo.shape[0]

    @pl.when(pl.program_id(0) == 0)
    def _():
        xf[0:half, :] = xo[...]
        xf[half:, :] = xt[...]
        if flip:
            nb = 256
            for at in range(0, xf.shape[1], nb):
                outs[-1][at : at + nb, :] = xf[:, at : at + nb].T

    w = weight_ref(ids, w, rest[-1])
    epi(ids, dot(xf[...], w[...]), extra, outs)


def nn_call(ids, xo, xt, w, col, steps, nb, epi, extra, outs, name, flip=False, us=5):
    half, width = xo.shape
    outs = list(outs)
    if flip:
        shape = (width, 2 * half)
        outs.append((shape, bf16, pl.BlockSpec(shape, lambda j, ids: (0, 0))))
    wi = weight_ins(w, width, nb, lambda j: col // nb + j)
    body = functools.partial(
        nn_kernel, n_w=len(wi), epi=epi, n_extra=len(extra), n_out=len(outs), flip=flip
    )
    return call(
        body,
        (steps,),
        [(xo, whole(xo)), (xt, whole(xt))] + wi + extra,
        outs,
        [pltpu.VMEM((2 * half, width), bf16)] + weight_scratch(w, width, nb),
        ids=ids,
        us=us,
        name=name,
    )


def epi_qkv(ids, y, extra, outs, *, base):
    (vec,) = extra
    j = pl.program_id(0)
    nb = y.shape[1]
    at = pl.multiple_of(ids[IC] * nb, nb)
    qb = vec[base + 2 : base + 3, pl.ds(at, nb)]
    vb = vec[base + 3 : base + 4, pl.ds(at, nb)]
    bias = jnp.where(j == 0, qb, jnp.where(j == 2, vb, 0.0))
    scale = jnp.where(j == 0, HD ** (-0.5), 1.0)
    outs[0][...] = ((y + bias) * scale).astype(bf16)


def gelu_parts(t):
    a = jnp.abs(t)
    k = 1.0 / (1.0 + 0.23164189 * a)
    e = jnp.exp(-0.5 * t * t)
    poly = k * (
        0.127414796 + k * (-0.142248368 + k * (0.7107068705 + k * (-0.7265760135 + k * 0.5307027145)))
    )
    tail = poly * e
    phi = jnp.where(t < 0, tail, 1.0 - tail)
    return phi, e * 0.3989422804014327


def epi_up(ids, y, extra, outs, *, base, own):
    (vec,) = extra
    j = pl.program_id(0)
    nb = y.shape[1]
    half = ids[IX] if own else 1 - ids[IX]
    row = base + 10 + 2 * ids[IC] + half
    bias = vec[pl.ds(row, 1), pl.ds(pl.multiple_of(j * nb, nb), nb)]
    u = y + bias
    phi, dens = gelu_parts(u)
    outs[0][...] = (u * phi).astype(bf16)
    outs[1][...] = (phi + u * dens).astype(bf16)


def epi_dact(ids, y, extra, outs):
    (gp,) = extra
    du = (y * gp[...].astype(f32)).astype(bf16)
    outs[0][...] = du
    outs[1][...] = col_sum(du.astype(f32))


def epi_plain(ids, y, extra, outs):
    outs[0][...] = y.astype(bf16)


def nt_kernel(ids, *rest, n_ws, epi, n_extra, n_out):
    n_in = sum(1 + n for n in n_ws)
    extra = rest[n_in : n_in + n_extra]
    outs = rest[n_in + n_extra : n_in + n_extra + n_out]
    acc = rest[n_in + n_extra + n_out]
    spares = rest[n_in + n_extra + n_out + 1 :]
    k = pl.program_id(0)
    nb = 256
    pairs = []
    at = 0
    for gi, n in enumerate(n_ws):
        spare = spares[gi] if spares else None
        pairs.append((rest[at], weight_ref(ids, rest[at + 1 : at + 1 + n], spare)))
        at += 1 + n

    def body(i, carry):
        cols = pl.ds(pl.multiple_of(i * nb, nb), nb)
        y = None
        for x, w in pairs:
            xv = x[...]
            v = dot(xv.reshape(xv.shape[-2:]), w[cols, :], NT)
            y = v if y is None else y + v

        @pl.when(k == 0)
        def _():
            acc[:, cols] = y

        @pl.when(k > 0)
        def _():
            acc[:, cols] += y

        return carry

    lax.fori_loop(0, acc.shape[1] // nb, body, 0)

    @pl.when(k == pl.num_programs(0) - 1)
    def _():
        epi(acc, extra, outs)


def nt_call(ids, groups, steps, kb, rows, wide, epi, extra, outs, name):
    ins, n_ws, scratch = [], [], [pltpu.VMEM((rows, wide), f32)]
    for x, xs, w, col in groups:
        ins.append((x, xs))
        wi = weight_ins(w, wide, kb, lambda k, c=col // kb: c + k)
        ins += wi
        n_ws.append(len(wi))
        scratch += weight_scratch(w, wide, kb)
    body = functools.partial(
        nt_kernel, n_ws=tuple(n_ws), epi=epi, n_extra=len(extra), n_out=len(outs)
    )
    return call(body, (steps,), ins + extra, outs, scratch, ids=ids, us=6, name=name)


def epi_send(acc, extra, outs):
    row_loop(acc.shape[0], lambda r: outs[0].__setitem__((r, slice(None)), acc[r, :].astype(bf16)))


def epi_proj(acc, extra, outs, *, base):
    recv, res, vec = extra
    mid_ref, branch_ref, h_ref = outs

    def fn(r):
        branch = acc[r, :] + recv[r, :].astype(f32) + vec[base + 4 : base + 5, :]
        mid = res[r, :].astype(f32) + vec[base + 5 : base + 6, :] * branch
        mid_ref[r, :] = mid
        branch_ref[r, :] = branch.astype(bf16)
        center, rstd = norm_stats(mid)
        h_ref[r, :] = (
            center * rstd * vec[base + 6 : base + 7, :] + vec[base + 7 : base + 8, :]
        ).astype(bf16)

    row_loop(acc.shape[0], fn)


def epi_down(acc, extra, outs, *, base, nxt):
    recv, mid, vec = extra
    out_ref, down_ref, h_ref = outs

    def fn(r):
        down = acc[r, :] + recv[r, :].astype(f32) + vec[base + 8 : base + 9, :]
        down_ref[r, :] = down.astype(bf16)
        res = mid[r, :] + vec[base + 9 : base + 10, :] * down
        out_ref[r, :] = res
        center, rstd = norm_stats(res)
        h_ref[r, :] = (
            center * rstd * vec[nxt : nxt + 1, :] + vec[nxt + 1 : nxt + 2, :]
        ).astype(bf16)

    row_loop(acc.shape[0], fn)


def epi_down_last(acc, extra, outs, *, base):
    recv, mid, vec, cot = extra
    out_ref, dd_ref, sums = outs
    sums[...] = jnp.zeros_like(sums)

    def fn(r):
        down = acc[r, :] + recv[r, :].astype(f32) + vec[base + 8 : base + 9, :]
        scale = vec[base + 9 : base + 10, :]
        out_ref[r, :] = mid[r, :] + scale * down
        g = cot[r, :].astype(f32)
        dd = (g * scale).astype(bf16)
        dd_ref[r, :] = dd
        sums[0:1, :] += col_sum(g * down)
        sums[1:2, :] += col_sum(dd.astype(f32))

    row_loop(acc.shape[0], fn)


def norm_back(grad, values, gain):
    center, rstd = norm_stats(values)
    n = center * rstd
    e = grad * gain
    me = jnp.mean(e, axis=-1, keepdims=True)
    men = jnp.mean(e * n, axis=-1, keepdims=True)
    return n, rstd * (e - me - n * men)


def epi_dh2(acc, extra, outs, *, base):
    recv, mid, g_in, branch, vec = extra
    dm_ref, db_ref, sums = outs
    sums[...] = jnp.zeros_like(sums)

    def fn(r):
        dh = acc[r, :] + recv[r, :].astype(f32)
        n, back = norm_back(dh, mid[r, :], vec[base + 6 : base + 7, :])
        dm = g_in[r, :].astype(f32) + back
        dm_ref[r, :] = dm
        db = (dm * vec[base + 5 : base + 6, :]).astype(bf16)
        db_ref[r, :] = db
        sums[0:1, :] += col_sum(dh * n)
        sums[1:2, :] += col_sum(dh)
        sums[2:3, :] += col_sum(dm * branch[r, :].astype(f32))
        sums[3:4, :] += col_sum(db.astype(f32))

    row_loop(acc.shape[0], fn)


def epi_dh1(acc, extra, outs, *, base, prev):
    if prev is None:
        recv, res, dm, vec = extra
        g_ref, sums = outs
    else:
        recv, res, dm, vec, down = extra
        g_ref, dd_ref, sums, dsums = outs
        dsums[...] = jnp.zeros_like(dsums)
    sums[...] = jnp.zeros_like(sums)

    def fn(r):
        dh = acc[r, :] + recv[r, :].astype(f32)
        n, back = norm_back(dh, res[r, :].astype(f32), vec[base : base + 1, :])
        g = dm[r, :] + back
        g_ref[r, :] = g
        sums[0:1, :] += col_sum(dh * n)
        sums[1:2, :] += col_sum(dh)
        if prev is not None:
            dd = (g * vec[prev + 9 : prev + 10, :]).astype(bf16)
            dd_ref[r, :] = dd
            dsums[0:1, :] += col_sum(g * down[r, :].astype(f32))
            dsums[1:2, :] += col_sum(dd.astype(f32))

    row_loop(acc.shape[0], fn)


def dw_kernel(ids, a_t, b, *rest, n_add, n_old, flat):
    y = dot(a_t[...], b[...].reshape(b.shape[-2:]))
    if n_add:
        y = y + rest[0][...].astype(f32)
    rest = rest[n_add + n_old :]
    if flat:
        rest[0][...] = y.astype(bf16)
        return
    keep, send, acc = rest
    acc[...] = y
    rows = keep.shape[1]
    for q in range(4):
        for bit, out in ((ids[IY], keep), (1 - ids[IY], send)):
            at = pl.multiple_of((2 * q + bit) * rows, rows)
            out[q] = acc[pl.ds(at, rows), :].astype(bf16)


def dw_call(ids, a_t, b, bspec, n, adds, name, flat=False, total=None, col=0, old=()):
    wide, tokens = a_t.shape
    nb = 256

    def cols(at):
        return pl.BlockSpec((wide, nb), lambda j, ids: (0, at // nb + j))

    if flat:
        outs = [((wide, total), bf16, cols(col))]
        scratch = []
    else:
        ospec = pl.BlockSpec((4, wide // 8, nb), lambda j, ids: (0, 0, col // nb + j))
        outs = [((4, wide // 8, total), bf16, ospec)] * 2
        scratch = [pltpu.VMEM((wide, nb), f32)]
    ins = [(a_t, whole(a_t)), (b, bspec)] + [(a, cols(at)) for a, at in adds]
    n_in = 1 + len(ins)
    ins += [(a, pl.BlockSpec(memory_space=pl.ANY)) for a in old]
    return call(
        functools.partial(dw_kernel, n_add=len(adds), n_old=len(old), flat=flat),
        (n // nb,),
        ins,
        outs,
        scratch,
        ids=ids,
        aliases={n_in + i: i for i in range(len(old))},
        name=name,
    )


def chunks_of(length):
    return [(s, min(256, length - s)) for s in range(0, length, 256)]


def head_lanes(rows, h):
    lane = lax.broadcasted_iota(jnp.int32, (rows, 2 * HD), 1)
    return (lane // HD) == h, lane == (1 - h) * HD


def attn_fwd_kernel(q_ref, k_ref, v_ref, mb_ref, o_ref, wide_ref, lse_ref):
    h = pl.program_id(0) % 2
    length = q_ref.shape[0]
    mine, mark = head_lanes(length, h)
    k0 = jnp.where(mine, k_ref[...].astype(f32), jnp.where(mark, mb_ref[...], 0.0)).astype(bf16)
    v_t = jnp.where(mine, v_ref[...].astype(f32), 1.0).astype(bf16).T
    for start, size in chunks_of(length):
        rows = pl.ds(start, size)
        mine_c, mark_c = head_lanes(size, h)
        q0 = jnp.where(mine_c, q_ref[rows, :].astype(f32), jnp.where(mark_c, 1.0, 0.0)).astype(bf16)
        s = dot(k0, q0, NT)
        top = jnp.max(s, axis=0, keepdims=True)
        p = jnp.exp(s - top).astype(bf16)
        o_t = dot(v_t, p)
        total = jnp.where(h == 0, o_t[HD : HD + 1, :], o_t[0:1, :])
        o = (o_t * (1.0 / total)).T
        o = jnp.where(mine_c, o, wide_ref[rows, :])
        wide_ref[rows, :] = o
        o_ref[rows, :] = o.astype(bf16)
        lse_ref[0, :, rows] = top + jnp.log(total)


def attn_fwd(qkv, mb):
    length, wide = qkv.shape
    pairs = wide // 3 // (2 * HD)
    blk = lambda off: pl.BlockSpec((length, 2 * HD), lambda g: (0, off + g // 2))
    return call(
        attn_fwd_kernel,
        (2 * pairs,),
        [(qkv, blk(0)), (qkv, blk(pairs)), (qkv, blk(2 * pairs)), (mb, whole(mb))],
        [
            ((length, wide // 3), bf16, blk(0)),
            ((length, wide // 3), f32, blk(0)),
            ((2 * pairs, 1, length), f32, pl.BlockSpec((1, 1, length), lambda g: (g, 0, 0))),
        ],
        us=30,
        name="attn_fwd",
    )


def attn_bwd_kernel(q_ref, k_ref, v_ref, do_ref, o_ref, mb_ref, lse_ref, g_ref, sums, dk_acc, dv_acc):
    h = pl.program_id(0) % 2
    length = q_ref.shape[0]
    mine, mark = head_lanes(length, h)
    kf = k_ref[...].astype(f32)
    k0 = jnp.where(mine, kf, jnp.where(mark, mb_ref[...], 0.0)).astype(bf16)
    k_t = k_ref[...].T
    v0 = jnp.where(mine, v_ref[...].astype(f32), 0.0).astype(bf16)
    for ci, (start, size) in enumerate(chunks_of(length)):
        rows = pl.ds(start, size)
        mine_c, mark_c = head_lanes(size, h)
        q = q_ref[rows, :]
        q0 = jnp.where(mine_c, q.astype(f32), jnp.where(mark_c, 1.0, 0.0)).astype(bf16)
        do = do_ref[rows, :]
        inner = jnp.where(mine_c, do.astype(f32) * o_ref[rows, :], 0.0)
        delta = jnp.sum(inner.T, axis=0, keepdims=True)
        p = jnp.exp(dot(k0, q0, NT) - lse_ref[0, :, rows])
        ds = (p * (dot(v0, do, NT) - delta)).astype(bf16)
        dv = dot(p.astype(bf16), do)
        dk = dot(ds, q)
        if ci == 0:
            dv_acc[...] = dv
            dk_acc[...] = dk
        else:
            dv_acc[...] += dv
            dk_acc[...] += dk
        dq = dot(k_t, ds).T * HD ** (-0.5)
        g_ref[0, rows, :] = jnp.where(mine_c, dq, g_ref[0, rows, :].astype(f32)).astype(bf16)
    g_ref[1] = jnp.where(mine, dk_acc[...], g_ref[1].astype(f32)).astype(bf16)
    g_ref[2] = jnp.where(mine, dv_acc[...], g_ref[2].astype(f32)).astype(bf16)

    @pl.when(h == 1)
    def _():
        sums[0] = col_sum(g_ref[0].astype(f32))
        sums[1] = col_sum(g_ref[2].astype(f32))


def attn_bwd(qkv, d_mixed, mixed, mb, lse):
    length, wide = qkv.shape
    pairs = wide // 3 // (2 * HD)
    blk = lambda off: pl.BlockSpec((length, 2 * HD), lambda g: (0, off + g // 2))
    return call(
        attn_bwd_kernel,
        (2 * pairs,),
        [
            (qkv, blk(0)),
            (qkv, blk(pairs)),
            (qkv, blk(2 * pairs)),
            (d_mixed, blk(0)),
            (mixed, blk(0)),
            (mb, whole(mb)),
            (lse, pl.BlockSpec((1, 1, length), lambda g: (g, 0, 0))),
        ],
        [
            (
                (3, length, wide // 3),
                bf16,
                pl.BlockSpec((3, length, 2 * HD), lambda g: (0, 0, g // 2)),
            ),
            ((2, 1, wide // 3), f32, pl.BlockSpec((2, 1, 2 * HD), lambda g: (0, 0, g // 2))),
        ],
        [pltpu.VMEM((length, 2 * HD), f32), pltpu.VMEM((length, 2 * HD), f32)],
        us=30,
        name="attn_bwd",
    )


def ln_kernel(x, vec, out, *, base):
    def fn(r):
        center, rstd = norm_stats(x[r, :].astype(f32))
        out[r, :] = (center * rstd * vec[base : base + 1, :] + vec[base + 1 : base + 2, :]).astype(bf16)

    row_loop(x.shape[0], fn)


def ln_call(x, vec, base):
    return call(
        functools.partial(ln_kernel, base=base),
        (1,),
        [(x, whole(x)), (vec, whole(vec))],
        [(x.shape, bf16, whole(x))],
        name="ln",
    )[0]


def vec_grad_kernel(ids, ln1, qv, ln2, down, ub_o, ub_t, out):
    out[...] = jnp.zeros_like(out)
    n = qv.shape[2]
    at = pl.multiple_of(ids[IC] * n, n)
    out[0:2, :] = ln1[0:2, :]
    out[2:3, pl.ds(at, n)] = qv[0]
    out[3:4, pl.ds(at, n)] = qv[1]
    out[4:5, :] = ln2[3:4, :]
    out[5:6, :] = ln2[2:3, :]
    out[6:8, :] = ln2[0:2, :]
    out[8:9, :] = down[1:2, :]
    out[9:10, :] = down[0:1, :]
    row = 10 + 2 * ids[IC]
    out[pl.ds(row + ids[IX], 1), :] = ub_o[...]
    out[pl.ds(row + 1 - ids[IX], 1), :] = ub_t[...]


def adam_math(w, g, m, v, rate, decay):
    m1 = B1 * m + (1.0 - B1) * g
    v1 = B2 * v + (1.0 - B2) * g * g
    step = -rate * (
        (m1 * (1.0 / (1.0 - B1**STEPS))) / (jnp.sqrt(v1 * (1.0 / (1.0 - B2**STEPS))) + ADAM_EPS)
        + decay * w.astype(f32)
    )
    return step, m1, v1


def adam_kernel(ids, *rest, pick, n_g, n_old):
    gs = rest[:n_g]
    w, m, v = rest[n_g : n_g + 3]
    g_out, s_out, m_out, v_out = rest[n_g + 3 + n_old :]
    g = pick(ids, pl.program_id(0), gs)
    step, m1, v1 = adam_math(w[0], g, m[0], v[0], RATE_M, DECAY)
    g_out[0] = g
    s_out[0] = step
    m_out[0] = m1
    v_out[0] = v1


def pick_attn(ids, b, gs):
    own, oth = [g[...].astype(f32) for g in gs]
    return jnp.where((b % 2) == ids[IC], own, oth)


def pick_mlp(ids, b, gs):
    own, oth = gs
    core = ((b // 2) % 2) == ids[IC]
    at = pl.ds(((b % 2) + ids[IX]) % 2, 1)
    return jnp.where(core, own[at][0].astype(f32), oth[at][0].astype(f32))


def adam_call(ids, layer, gs, gspecs, w, m, v, nb, pick, old, name):
    spec = pl.BlockSpec((1, w.shape[1], nb), lambda b, ids: (layer, 0, b))
    ins = list(zip(gs, gspecs)) + [(w, spec), (m, spec), (v, spec)]
    n_in = len(ins) + 1
    ins += [(o, pl.BlockSpec(memory_space=pl.ANY)) for o in old]
    return call(
        functools.partial(adam_kernel, pick=pick, n_g=len(gs), n_old=len(old)),
        (w.shape[2] // nb,),
        ins,
        [(w.shape, f32, spec)] * 4,
        ids=ids,
        aliases={n_in + i: i for i in range(len(old))},
        name=name,
    )


def copy_kernel(ids, a, out):
    out[...] = a[0]


def pick_columns(ids, a, layer, nb, steps, index, name):
    rows = a.shape[1]
    return call(
        copy_kernel,
        (steps,),
        [(a, pl.BlockSpec((1, rows, nb), lambda j, ids: (layer, 0, index(j, ids))))],
        [((rows, nb * steps), bf16, pl.BlockSpec((rows, nb), lambda j, ids: (0, j)))],
        ids=ids,
        name=name,
    )[0]


SWAP = [(0, 1), (1, 0)]


def swap_core(a):
    return lax.ppermute(a, "seq", SWAP)


def swap_x(a):
    return lax.ppermute(a, "dp", SWAP)


def swap_bit(a, bit):
    return lax.ppermute(a, "fsdp", [(i, i ^ bit) for i in range(8)])


def merge_kernel(ids, own, recv, out, *, bit):
    mine = pl.program_id(1) == ids[bit]

    @pl.when(mine)
    def _():
        out[0] = own[...]

    @pl.when(jnp.logical_not(mine))
    def _():
        out[0] = recv[...]


def merge(ids, own, recv, bit):
    a, b, n = own.shape
    ins = pl.BlockSpec((1, b, n), lambda i, j, ids: (i, 0, 0))
    (out,) = call(
        functools.partial(merge_kernel, bit=bit),
        (a, 2),
        [(own, ins), (recv, ins)],
        [((a, 2, b, n), own.dtype, pl.BlockSpec((1, 1, b, n), lambda i, j, ids: (i, j, 0, 0)))],
        ids=ids,
        name="merge",
    )
    return out.reshape(2 * a, b, n)


def merge_z_kernel(ids, *rest):
    out = rest[-1]
    z = 2 * ids[IZ1] + ids[IZ0]
    for k, part in enumerate(rest[:-1]):
        out[pl.ds((z - k + 4) % 4, 1)] = part[...][None]


def gather_z(ids, own):
    parts = [own] + [
        lax.ppermute(own, "fsdp", [(i, (i + 2 * k) % 8) for i in range(8)]) for k in range(1, 4)
    ]
    b, n = own.shape
    nb = 512
    ins = pl.BlockSpec((b, nb), lambda j, ids: (0, j))
    return call(
        merge_z_kernel,
        (n // nb,),
        [(p, ins) for p in parts],
        [((4, b, n), own.dtype, pl.BlockSpec((4, b, nb), lambda j, ids: (0, 0, j)))],
        ids=ids,
        name="merge_z",
    )[0]


def fold_kernel(ids, keep, recv, keep_out, send_out, *, bit):
    for a in range(keep_out.shape[0]):
        for b, out in ((ids[bit], keep_out), (1 - ids[bit], send_out)):
            at = 2 * a + b
            v = keep[pl.ds(at, 1)].astype(f32) + recv[pl.ds(at, 1)].astype(f32)
            out[a] = v[0].astype(bf16)


def fold(ids, keep, recv, bit):
    a, b, n = keep.shape
    nb = 512
    ins = pl.BlockSpec((a, b, nb), lambda j, ids: (0, 0, j))
    outs = pl.BlockSpec((a // 2, b, nb), lambda j, ids: (0, 0, j))
    return call(
        functools.partial(fold_kernel, bit=bit),
        (n // nb,),
        [(keep, ins), (recv, ins)],
        [((a // 2, b, n), bf16, outs)] * 2,
        ids=ids,
        name="fold",
    )


def apart(go, fn, *args):
    def empty(*args):
        return jax.tree.map(lambda v: jnp.zeros(v.shape, v.dtype), jax.eval_shape(fn, *args))

    return lax.cond(go, fn, empty, *args)


def tie(*arrays):
    return lax.optimization_barrier(arrays)


def local(
    tokens_in,
    key_mask,
    attn_weights,
    mlp_weights,
    vectors,
    cotangent,
    first_attn,
    second_attn,
    first_mlp,
    second_mlp,
    first_vec,
    second_vec,
):
    layers, shard, _ = attn_weights.shape
    n_fsdp = lax.axis_size("fsdp")
    staged = n_fsdp == 8
    c = lax.axis_index("seq")
    x = lax.axis_index("dp")
    f = lax.axis_index("fsdp")
    ids = jnp.stack([f // 4 % 2, f // 2 % 2, f % 2, c, x]).astype(jnp.int32)

    tokens = tokens_in[0]
    go = key_mask[0, 0] >= 0
    cot = cotangent[0]
    half, wide = tokens.shape
    length = 2 * half
    group = wide // 2
    bias = jnp.where(key_mask[0] > 0, 0.0, -1e30).astype(f32).reshape(2, half)
    bias = jnp.where(c == 0, bias, bias[::-1]).reshape(length, 1)
    mb = jnp.broadcast_to(bias, (length, 2 * HD))

    pa = [
        pick_columns(ids, attn_weights, l, group, 4, lambda j, ids: 2 * j + ids[IC], "pick_a")
        for l in range(layers)
    ]
    pm = [
        pick_columns(
            ids, mlp_weights, l, wide, 2, lambda j, ids: 4 * j + 2 * ids[IC] + ids[IX], "pick_m"
        )
        for l in range(layers)
    ]
    pv = vectors.reshape(1, layers * ROWS, -1)
    def line(p, bits):
        for bit, at in bits:
            p = merge(ids, p, swap_bit(p, bit), at)
        return p

    Z1, Z0, Y = (4, IZ1), (2, IZ0), (1, IY)
    if staged:
        vec = line(pv, (Z1, Z0, Y))
    else:
        vec = lax.all_gather(pv, "fsdp", axis=0, tiled=True)
    vec = vec.transpose(1, 0, 2).reshape(layers * ROWS, -1).astype(f32)

    h_own = ln_call(tokens, vec, 0)
    h_own, *pm = tie(h_own, *pm)
    h_oth = apart(go, swap_core, h_own)
    wa, wm = [None] * layers, [None] * layers
    for l in range(layers):
        a = pa[l]
        if staged and l == 1:
            a, z4 = tie(a, z4)
        wa[l] = lax.all_gather(a, "fsdp", axis=0, tiled=True)
        if not staged:
            w = lax.all_gather(pm[l], "fsdp", axis=0, tiled=True)
            wm[l] = [w, swap_x(w)]
        elif l == 0:
            z4 = gather_z(ids, pm[0])

    vspec = pl.BlockSpec(vec.shape, lambda *_: (0, 0))
    V = (vec, vspec)
    own = pl.BlockSpec((half, wide), lambda *_: (0, 0))

    def xs(row, kb):
        return pl.BlockSpec((half, kb), lambda k, ids: (row, k))

    def fixed(shape):
        return pl.BlockSpec(shape, lambda *_: (0,) * len(shape))

    KB = 512
    nb = 256
    colspec = pl.BlockSpec((length, nb), lambda j, ids: (0, j))
    send_out = [((half, wide), bf16, own)]
    res = tokens
    saved = []
    for l in range(layers):
        base = l * ROWS
        if staged and l == 0:
            h_oth, z4 = tie(h_oth, z4)
            y0 = swap_bit(z4, 1)
            far_a = swap_x(z4)
            pm_next, _ = tie(pm[1][None], z4)
        if staged and l == 1:
            h_oth, y1 = tie(h_oth, y1)
            z4 = m_four
        qkv, h_t = nn_call(
            ids, h_own, h_oth, wa[l], 0, 3, group, functools.partial(epi_qkv, base=base), [V],
            [((length, 3 * group), bf16, pl.BlockSpec((length, group), lambda j, ids: (0, j)))],
            "qkv", flip=True,
        )
        if staged and l == 1:
            qkv, far_a = tie(qkv, far_a)
        mixed, mixed_wide, lse = attn_fwd(qkv, mb)
        if staged and l == 0:
            m_recv = swap_bit(pm_next, 4)
            mixed, y0, far_a, m_recv = tie(mixed, y0, far_a, m_recv)
            wm[0] = [(z4, y0), (far_a, swap_x(y0))]
            m_two = merge(ids, pm_next, m_recv, IZ1)
            m_recv = swap_bit(m_two, 2)
        if staged and l == 1:
            far_b = swap_x(y1)
            mixed, far_b = tie(mixed, far_b)
            wm[1] = [(z4, y1), (far_a, far_b)]

        def proj_pair(mixed, w, res, vec):
            def proj(row, epi, extra, outs):
                return nt_call(
                    ids, [(mixed, xs(row, KB), w, 3 * group)], group // KB, KB, half, wide, epi,
                    extra, outs, "proj",
                )

            (part,) = proj(1, epi_send, [], send_out)
            mid, branch, h2_own = proj(
                0, functools.partial(epi_proj, base=base),
                [(swap_core(part), own), (res, own), (vec, vspec)],
                [((half, wide), f32, own), ((half, wide), bf16, own), ((half, wide), bf16, own)],
            )
            return mid, branch, h2_own, swap_core(h2_own)

        mid, branch, h2_own, h2_oth = apart(go, proj_pair, mixed, wa[l], res, vec)
        act, gp = [], []
        for i in (0, 1):
            if staged and l == 0 and i == 1:
                h2_own, m_recv = tie(h2_own, m_recv)
                m_four = merge(ids, m_two, m_recv, IZ0)
                y1 = swap_bit(m_four, 1)
                far_a = swap_x(m_four)
            got = nn_call(
                ids, h2_own, h2_oth, wm[l][i], 0, wide // nb, nb,
                functools.partial(epi_up, base=base, own=i == 0), [V],
                [((length, wide), bf16, colspec)] * 2, "up", flip=i == 0,
            )
            act.append(got[0])
            gp.append(got[1])
            if i == 0:
                h2_t = got[2]

        last = l == layers - 1

        def down_pair(act, wm, mid, vec, cot):
            def down(row, epi, extra, outs):
                return nt_call(
                    ids, [(act[i], xs(row, KB), wm[i], wide) for i in (0, 1)],
                    wide // KB, KB, half, wide, epi, extra, outs, "down",
                )

            (part,) = down(1, epi_send, [], send_out)
            recv = swap_core(part)
            if last:
                out, dd_own, dsums = down(
                    0, functools.partial(epi_down_last, base=base),
                    [(recv, own), (mid, own), (vec, vspec), (cot, own)],
                    [((half, wide), f32, own), ((half, wide), bf16, own), ((2, wide), f32, fixed((2, wide)))],
                )
                return out, dd_own, dsums, swap_core(dd_own)
            out, down_out, h_next = down(
                0, functools.partial(epi_down, base=base, nxt=base + ROWS),
                [(recv, own), (mid, own), (vec, vspec)],
                [((half, wide), f32, own), ((half, wide), bf16, own), ((half, wide), bf16, own)],
            )
            return out, h_next, down_out, swap_core(h_next)

        out, next_own, extra_out, next_oth = apart(go, down_pair, act, wm[l], mid, vec, cot)
        if last:
            dd_own, dd_oth, dsums, down_out = next_own, next_oth, extra_out, None
        else:
            down_out = extra_out
        saved.append((res, h_t, qkv, mixed, mixed_wide, lse, mid, branch, h2_t, act, gp, down_out))
        if not last:
            res, h_own, h_oth = out, next_own, next_oth
    tokens_out = out

    g = cot
    old_a, old_m = [], []
    gvecs = [None] * layers
    pend = {}

    def step_y(key, parts):
        if staged:
            pend[key] = (parts[0], swap_bit(parts[1], 1))
        else:
            pend[key] = lax.psum_scatter(parts[0], "fsdp", scatter_dimension=0, tiled=True)

    def tied(key, other):
        other, pend[key] = tie(other, pend[key])
        return other

    def step_z0(key):
        keep, send = fold(ids, *pend[key], IZ0)
        pend[key] = (keep, swap_bit(send, 2))

    def step_z1(key):
        keep, send = fold(ids, *pend[key], IZ1)
        pend[key] = (keep, swap_bit(send, 4))

    def step_end(key):
        keep, recv = pend[key]
        return keep[0].astype(f32) + recv[0].astype(f32)

    for l in reversed(range(layers)):
        base = l * ROWS
        lower = l > 0
        split = not lower
        flat = lower or not staged
        res, h_t, qkv, mixed, mixed_wide, lse, mid, branch, h2_t, act, gp, _ = saved[l]
        du, ub = [None, None], [None, None]
        for i in (1, 0):
            got = nn_call(
                ids, dd_own, dd_oth, wm[l][i], wide, wide // nb, nb, epi_dact,
                [(gp[i], colspec)],
                [((length, wide), bf16, colspec), ((1, wide), f32, pl.BlockSpec((1, nb), lambda j, ids: (0, j)))],
                "dact", flip=i == 1,
            )
            du[i], ub[i] = got[:2]
            if i == 1:
                dd_t = got[2]
                if split:
                    far = []
                    for a_t, b in ((h2_t, du[1]), (dd_t, act[1])):
                        far += dw_call(ids, a_t, b, colspec, wide, [], "dw_far", flat=True, total=wide)
                    dd_own, *_ = tie(dd_own, *far)
                    far = [swap_x(v) for v in far]
        if not split:
            d_m = ()
            for n, (a_t, b) in enumerate(((h2_t, du[0]), (dd_t, act[0]), (h2_t, du[1]), (dd_t, act[1]))):
                d_m = dw_call(
                    ids, a_t, b, colspec, wide, [], "dw_mlp", flat=True, total=4 * wide, col=n * wide, old=d_m
                )
            du[0], d_m = tie(du[0], d_m[0])
            pend[("m", l)] = lax.psum_scatter(d_m, "fsdp", scatter_dimension=0, tiled=True)

        def dh2_pair(du, wm, mid, g, branch, vec):
            def dh2(row, epi, extra, outs):
                return nt_call(
                    ids, [(du[i], xs(row, KB), wm[i], 0) for i in (0, 1)],
                    wide // KB, KB, half, wide, epi, extra, outs, "dh2",
                )

            (part,) = dh2(1, epi_send, [], send_out)
            dm, db_own, sums2 = dh2(
                0, functools.partial(epi_dh2, base=base),
                [(swap_core(part), own), (mid, own), (g, own), (branch, own), (vec, vspec)],
                [((half, wide), f32, own), ((half, wide), bf16, own), ((4, wide), f32, fixed((4, wide)))],
            )
            return dm, db_own, sums2, swap_core(db_own)

        dm, db_own, sums2, db_oth = apart(go, dh2_pair, du, wm[l], mid, g, branch, vec)
        if split:
            db_oth, pend[("m", l + 1)] = tie(db_oth, pend[("m", l + 1)])
            d_up, _ = tie(pend[("a", l + 1)], pend[("m", l + 1)])
            pend[("a", l + 1)] = lax.psum_scatter(d_up, "fsdp", scatter_dimension=0, tiled=True)
        d_mixed, db_t = nn_call(
            ids, db_own, db_oth, wa[l], 3 * group, group // nb, nb, epi_plain, [],
            [((length, group), bf16, colspec)], "dmixed", flip=True,
        )
        d_a = dw_call(
            ids, db_t, mixed, colspec, group, [], "dw_p", flat=flat, total=4 * group, col=3 * group
        )
        d_mixed, d_a = tie(d_mixed, d_a)
        d_qkv, qv = attn_bwd(qkv, d_mixed, mixed_wide, mb, lse)
        qspec = pl.BlockSpec((1, length, nb), lambda j, ids: (j * nb // group, 0, j % (group // nb)))
        d_a = dw_call(
            ids, h_t, d_qkv, qspec, 3 * group, [], "dw_qkv", flat=flat, total=4 * group, old=d_a
        )
        d_qkv, d_a = tie(d_qkv, d_a)
        if not split:
            pend[("a", l)] = d_a[0]
        else:
            step_y("a", d_a)
            d_qkv, *far = tie(d_qkv, *far)
            near = ()
            for n, (a_t, b) in enumerate(((h2_t, du[0]), (dd_t, act[0]))):
                near = dw_call(
                    ids, a_t, b, colspec, wide, [(far[n], 0)], "dw_near", flat=flat,
                    total=2 * wide, col=n * wide, old=near,
                )
            d_qkv, near = tie(d_qkv, near)
            step_y("m", near)
        down_below = saved[l - 1][-1] if lower else None

        def dh1_pair(d_qkv, w, res, dm, vec, down_below):
            def dh1(row, epi, extra, outs):
                spec = pl.BlockSpec((1, half, group), lambda k, ids: (k, row, 0))
                return nt_call(ids, [(d_qkv, spec, w, 0)], 3, group, half, wide, epi, extra, outs, "dh1")

            (part,) = dh1(1, epi_send, [], send_out)
            extra = [(swap_core(part), own), (res, own), (dm, own), (vec, vspec)]
            outs = [((half, wide), f32, own), ((2, wide), f32, fixed((2, wide)))]
            if lower:
                extra.append((down_below, own))
                outs[1:1] = [((half, wide), bf16, own)]
                outs.append(((2, wide), f32, fixed((2, wide))))
            got = dh1(0, functools.partial(epi_dh1, base=base, prev=base - ROWS if lower else None), extra, outs)
            return got, swap_core(got[1]) if lower else ()

        got, below_oth = apart(go, dh1_pair, d_qkv, wa[l], res, dm, vec, down_below)
        sums1 = got[2] if lower else got[1]

        (gvecs[l],) = call(
            vec_grad_kernel,
            (1,),
            [(a, whole(a)) for a in (sums1, qv, sums2, dsums, ub[0], ub[1])],
            [((16, wide), f32, fixed((16, wide)))],
            ids=ids,
            name="vec_grad",
        )
        g = got[0]
        if lower:
            dd_own, dd_oth, dsums = got[1], below_oth, got[3]
    grad_tokens = g

    for l in reversed(range(layers)):
        if l == 0 and staged:
            pend["a"], old_a, old_m = tie(pend["a"], tuple(old_a), tuple(old_m))
            for step in (step_z0, step_z1):
                for key in ("a", "m"):
                    step(key)
            g_a, g_m = step_end("a").astype(bf16), step_end("m").astype(bf16)
        elif l == 0:
            g_a, g_m = pend["a"], pend["m"]
        else:
            g_a, g_m = pend[("a", l)], pend[("m", l)]
        g_a = (g_a.astype(f32) + swap_x(g_a).astype(f32)).astype(bf16)
        if l > 0:
            r_m = swap_x(g_m)
            n = 2 * wide
            g_m = jnp.stack(
                [
                    (g_m[:, :n].astype(f32) + r_m[:, n:].astype(f32)).astype(bf16),
                    (g_m[:, n:].astype(f32) + r_m[:, :n].astype(f32)).astype(bf16),
                ]
            )
        else:
            g_m = jnp.stack([g_m, swap_x(g_m)])
        g_mt = swap_core(g_m)
        g_at = swap_core(g_a)
        aspec = pl.BlockSpec((shard, group), lambda b, ids: (0, b // 2))
        old_a = adam_call(
            ids, l, [g_a, g_at], [aspec, aspec], attn_weights, first_attn, second_attn,
            group, pick_attn, old_a, "adam_attn",
        )
        mspec = pl.BlockSpec((2, shard, wide), lambda b, ids: (0, 0, b // 4))
        old_m = adam_call(
            ids, l, [g_m, g_mt], [mspec] * 2, mlp_weights, first_mlp, second_mlp,
            wide, pick_mlp, old_m, "adam_mlp",
        )

    gv = jnp.stack(gvecs)
    if staged:
        gv = gv + swap_core(gv)
        gv = gv + swap_x(gv)
        for bit in (1, 2, 4):
            gv = gv + swap_bit(gv, bit)
    else:
        gv = lax.psum(gv, ("dp", "fsdp", "seq"))
    gv = lax.dynamic_slice_in_dim(gv, f * (wide // n_fsdp), wide // n_fsdp, axis=2)
    gv = gv[:, :ROWS]
    step_v, one_v, two_v = adam_math(vectors, gv, first_vec, second_vec, RATE_V, 0.0)

    return (
        tokens_out[None],
        grad_tokens[None],
        old_a[0],
        old_m[0],
        gv,
        old_a[1],
        old_m[1],
        step_v,
        old_a[2],
        old_a[3],
        old_m[2],
        old_m[3],
        one_v,
        two_v,
    )


def solution(mesh):
    tok = P(("dp", "fsdp"), "seq", None)
    mat = P(None, "fsdp", None)
    vec = P(None, None, "fsdp")
    return jax.shard_map(
        local,
        mesh=mesh,
        in_specs=(tok, P(("dp", "fsdp"), None), mat, mat, vec, tok, mat, mat, mat, mat, vec, vec),
        out_specs=(tok, tok, mat, mat, vec, mat, mat, vec, mat, mat, mat, mat, vec, vec),
        check_vma=False,
    )
```

time: 2320 us -> 930 us (0.40)
  waiting for transfers between devices: 1320 us -> 332 us
  matrix products: 486 us -> 0 us
  Pallas kernels: 0 us -> 468 us
  local copies, waits for them, and re-layouts: 247 us -> 34.9 us
  other arithmetic: 136 us -> 5.36 us
  blocking collectives: 101 us -> 0 us
  starting transfers between devices: 0.62 us -> 63.2 us
    reduce_scatter x4 -> x2, waiting for transfers between devices: 781 us -> 0.02 us  [the longest x1 0.02 us: local(): lax.psum_scatter(d_m, 'fsdp', scatter_dimension=0, tiled=True)]
    dot_general x136 -> x0, matrix products: 486 us -> none  [the longest x56 176 us: contract_last(): lax.dot_general(left_side, right_side, (((left_side.ndim - 1,), (1,)), ((...]
    pallas_call x0 -> x65, Pallas kernels: none -> 468 us  [call(): pl.pallas_call(body, out_shape=[sds(sh, dt) for sh, dt, _ in outs], grid_...]
    ppermute x0 -> x51, waiting for transfers between devices: none -> 330 us  [the longest x16 128 us: swap_bit(): return lax.ppermute(a, 'fsdp', [(i, i ^ bit) for i in range(8)])]
    all_gather x4 -> x2, waiting for transfers between devices: 297 us -> 1.87 us  [local(): wa[l] = lax.all_gather(a, 'fsdp', axis=0, tiled=True)]
    unnamed x13 -> x4, waiting for transfers between devices: 125 us -> 0.07 us
    psum x1 -> x0, waiting for transfers between devices: 113 us -> none  [local(): lax.psum(owned[0].astype(jnp.bfloat16), ('dp', 'seq')).astype(jnp.float32)]
    reshape x19 -> x1, local copies, waits for them, and re-layouts: 71.8 us -> 0.01 us  [local(): pv = vectors.reshape(1, layers * ROWS, -1)]
  transfers between devices with their start and end apart: 11 -> 55, of which waited for: 11 -> 36; matrix products, arithmetic and copies ran while one was open for 17% -> 1% of each run, Pallas kernels for 0% -> 41%
where the time goes in v1:
time: 930 us; the launch traced here: 922 us
  Pallas kernels  468 us (50%)
  waiting for transfers between devices  332 us (36%)
  starting transfers between devices  63.2 us (7%)
  local copies, waits for them, and re-layouts  34.9 us (4%)
  between operations  16.3 us (2%)
    pallas_call x65, Pallas kernels, call(): pl.pallas_call(body, out_shape=[sds(sh, dt) for sh, dt, _ in outs], grid_...  468 us
    ppermute x16, waiting for transfers between devices, swap_bit(): return lax.ppermute(a, 'fsdp', [(i, i ^ bit) for i in range(8)])  128 us
    ppermute x11, waiting for transfers between devices, swap_x(): return lax.ppermute(a, 'dp', SWAP)  91.3 us
    ppermute x3, waiting for transfers between devices, gather_z(): lax.ppermute(own, 'fsdp', [(i, (i + 2 * k) % 8) for i in range(8)])  66.6 us
    ppermute x21, waiting for transfers between devices, swap_core(): return lax.ppermute(a, 'seq', SWAP)  43.9 us
    ppermute x16, starting transfers between devices, swap_bit(): return lax.ppermute(a, 'fsdp', [(i, i ^ bit) for i in range(8)])  41.3 us
    unnamed x173, local copies, waits for them, and re-layouts  33.7 us
  transfers between devices with their start and end apart: 55, of which 36 were waited for; matrix products, arithmetic and copies ran while one was open for 1% of the time, Pallas kernels for 41%

profile of v1, /device:TPU:0, one launch (start us, length us, event | category | flops | bytes accessed | tf_op | source)
XLA Modules:
  0.0 922.0 jit_solution(2500701479793397102)
XLA Ops:
  53.0 55.8 %collective-permute-done.20.rest_2_ = bf16[128,2048]{1,0:T(8,128)(2,1)S(1)} collective-permute-done((bf16[128,2048]{1,0:T(8,128)(2,1)S(1)}, bf16[128,2048]{1,0:T(8,128)(2,1)S(1)}, u32[]{:S(2)}, u32[]{:S(2)}) %collective-permute-start.20) | collective-permute-done | bytes 524320 | tf_op jit(solution)/shard_map/ppermute | solution.py:675
  131.1 30.8 %attn_fwd.2 = (bf16[1040,512]{1,0:T(8,128)(2,1)S(1)}, f32[1040,512]{1,0:T(8,128)S(1)}, f32[8,1,1040]{2,1,0:T(1,128)S(1)}) custom-call(bf16[1040,1536]{1,0:T(8,128)(2,1)S(1)} %get-tuple-element.395.q_ref.k_ref.v_ref, bf16[1040,1536]{1,0:T(8,128)(2,1)S(1)} %get-tuple-element.395.q_ref.k_ref.v_ref, bf16[1040,1536]{1,0:T(8,128)(2,1)S(1)} %get-tuple-element.395.q_ref.k_ref.v_ref, ...), custom_call_target="tpu_custom_call" | custom-call | flops 1 | bytes 1 | tf_op jit(solution)/shard_map/attn_fwd/pallas_call | solution.py:44
  166.9 18.5 %collective-permute-start.25 = (bf16[2,128,2048]{2,1,0:T(8,128)(2,1)}, bf16[2,128,2048]{2,1,0:T(8,128)(2,1)}, u32[]{:S(2)}, u32[]{:S(2)}) collective-permute-start(bf16[2,128,2048]{2,1,0:T(8,128)(2,1)} %bitcast.14.own), channel_id=1, source_target_pairs={{0,4},{2,6},{4,0},{6,2},{8,12},{10,14},{12,8},{14,10},{1,5},{3,7},... | collective-permute-start | bytes 3145736 | tf_op jit(solution)/shard_map/ppermute | solution.py:637
  186.1 13.3 %conditional.10 = (f32[520,1024]{1,0:T(8,128)}, bf16[520,1024]{1,0:T(8,128)(2,1)}, bf16[520,1024]{1,0:T(8,128)(2,1)}, bf16[520,1024]{1,0:T(8,128)(2,1)}) conditional(s32[]{:T(128)} %bitcast.2, () %tuple.105, (s32[5]{0:T(128)S(1)}, bf16[1040,512]{1,0:T(8,128)(2,1)S(1)}, bf16[1024,2048]{1,0:T(8,128)(2,1)S(1)}, bf16[520,1024]{1,0:T(8,128)(2,1)S(1)}, ...), branch_computations={%region_2.3_spmd, %region_3.4_spmd} | conditional | flops 2 | bytes 8519794 | solution.py:717
  199.4 37.2 %collective-permute-done.25.recv = bf16[2,128,2048]{2,1,0:T(8,128)(2,1)} collective-permute-done((bf16[2,128,2048]{2,1,0:T(8,128)(2,1)}, bf16[2,128,2048]{2,1,0:T(8,128)(2,1)}, u32[]{:S(2)}, u32[]{:S(2)}) %collective-permute-start.25) | collective-permute-done | bytes 1048608 | tf_op jit(solution)/shard_map/ppermute | solution.py:637
  266.1 22.7 %conditional.11 = (f32[520,1024]{1,0:T(8,128)}, bf16[520,1024]{1,0:T(8,128)(2,1)}, bf16[520,1024]{1,0:T(8,128)(2,1)}, bf16[520,1024]{1,0:T(8,128)(2,1)}) conditional(s32[]{:T(128)} %bitcast.2, () %tuple.104, (s32[5]{0:T(128)S(1)}, bf16[1040,1024]{1,0:T(8,128)(2,1)S(1)}, bf16[4,128,2048]{2,1,0:T(8,128)(2,1)}, bf16[4,128,2048]{2,1,0:T(8,128)(2,1)}, ...), branch_computations={%region_4.5_spmd, %region_5.6_spmd} | conditional | flops 2 | bytes 8519794 | solution.py:717
  302.4 30.7 %attn_fwd.3 = (bf16[1040,512]{1,0:T(8,128)(2,1)S(1)}, f32[1040,512]{1,0:T(8,128)S(1)}, f32[8,1,1040]{2,1,0:T(1,128)S(1)}) custom-call(bf16[1040,1536]{1,0:T(8,128)(2,1)S(1)} %get-tuple-element.416.q_ref.k_ref.v_ref, bf16[1040,1536]{1,0:T(8,128)(2,1)S(1)} %get-tuple-element.416.q_ref.k_ref.v_ref, bf16[1040,1536]{1,0:T(8,128)(2,1)S(1)} %get-tuple-element.416.q_ref.k_ref.v_ref, ...), custom_call_target="tpu_custom_call" | custom-call | flops 1 | bytes 1 | tf_op jit(solution)/shard_map/attn_fwd/pallas_call | solution.py:44
  333.2 12.6 %collective-permute-done.29.rest_1_ = bf16[4,128,2048]{2,1,0:T(8,128)(2,1)} collective-permute-done((bf16[4,128,2048]{2,1,0:T(8,128)(2,1)}, bf16[4,128,2048]{2,1,0:T(8,128)(2,1)}, u32[]{:S(2)}, u32[]{:S(2)}) %collective-permute-start.29) | collective-permute-done | bytes 2097184 | tf_op jit(solution)/shard_map/ppermute | solution.py:633
  345.8 14.9 %conditional.12 = (f32[520,1024]{1,0:T(8,128)}, bf16[520,1024]{1,0:T(8,128)(2,1)}, bf16[520,1024]{1,0:T(8,128)(2,1)}, bf16[520,1024]{1,0:T(8,128)(2,1)}) conditional(s32[]{:T(128)} %bitcast.2, () %tuple.103, (s32[5]{0:T(128)S(1)}, bf16[1040,512]{1,0:T(8,128)(2,1)S(1)}, bf16[1024,2048]{1,0:T(8,128)(2,1)S(1)}, f32[520,1024]{1,0:T(8,128)}, ...), branch_computations={%region_6.7_spmd, %region_7.8_spmd} | conditional | flops 2 | bytes 8519794 | solution.py:717
  384.5 22.3 %conditional.13 = (bf16[520,1024]{1,0:T(8,128)(2,1)}, f32[2,1024]{1,0:T(2,128)S(1)}, bf16[520,1024]{1,0:T(8,128)(2,1)}, f32[1,520,1024]{2,1,0:T(8,128)}) conditional(s32[]{:T(128)} %bitcast.2, () %tuple.102, (s32[5]{0:T(128)S(1)}, bf16[1040,1024]{1,0:T(8,128)(2,1)S(1)}, bf16[4,128,2048]{2,1,0:T(8,128)(2,1)}, bf16[4,128,2048]{2,1,0:T(8,128)(2,1)}, ...), branch_computations={%region_8.9_spmd, %region_9.10_spmd} | conditional | flops 2 | bytes 8519794 | solution.py:717
  443.9 24.4 %conditional.14 = (f32[520,1024]{1,0:T(8,128)}, bf16[520,1024]{1,0:T(8,128)(2,1)}, f32[4,1024]{1,0:T(4,128)S(1)}, bf16[520,1024]{1,0:T(8,128)(2,1)}) conditional(s32[]{:T(128)} %bitcast.2, () %tuple.123, (s32[5]{0:T(128)S(1)}, bf16[1040,1024]{1,0:T(8,128)(2,1)}, bf16[4,128,2048]{2,1,0:T(8,128)(2,1)}, bf16[4,128,2048]{2,1,0:T(8,128)(2,1)}, ...), branch_computations={%region_10.11_spmd, %region_11.12_spmd} | conditional | flops 2 | bytes 42598652 | solution.py:717
  475.7 30.0 %attn_bwd.2 = (bf16[3,1040,512]{2,1,0:T(8,128)(2,1)S(1)}, f32[2,1,512]{2,1,0:T(1,128)S(1)}) custom-call(bf16[1040,1536]{1,0:T(8,128)(2,1)S(1)} %copy-done.2, bf16[1040,1536]{1,0:T(8,128)(2,1)S(1)} %copy-done.2, bf16[1040,1536]{1,0:T(8,128)(2,1)S(1)} %copy-done.2, bf16[1040,512]{1,0:T(8,128)(2,1)S(1)} %get-tuple-element.443.do_ref, ...), custom_call_target="tpu_custom_call" | custom-call | flops 1 | bytes 1 | tf_op jit(solution)/shard_map/attn_bwd/pallas_call | solution.py:44
  515.8 25.4 %conditional.15 = (f32[520,1024]{1,0:T(8,128)}, bf16[520,1024]{1,0:T(8,128)(2,1)}, f32[2,1024]{1,0:T(2,128)S(1)}, f32[2,1024]{1,0:T(2,128)S(1)}, bf16[520,1024]{1,0:T(8,128)(2,1)}) conditional(s32[]{:T(128)} %bitcast.2, () %tuple.122, (s32[5]{0:T(128)S(1)}, bf16[3,1040,512]{2,1,0:T(8,128)(2,1)}, bf16[1024,2048]{1,0:T(8,128)(2,1)}, ...), branch_computations={%region_12.13_spmd, %region_13.14_spmd} | conditional | flops 2 | bytes 38076592 | solution.py:717
  525.7 12.2 %dh1.5 = (f32[520,1024]{1,0:T(8,128)}, bf16[520,1024]{1,0:T(8,128)(2,1)}, f32[2,1024]{1,0:T(2,128)S(1)}, f32[2,1024]{1,0:T(2,128)S(1)}) custom-call(s32[5]{0:T(128)S(1)} %get-tuple-element.191.ids, bf16[3,1040,512]{2,1,0:T(8,128)(2,1)S(1)} %copy-done.54, bf16[1024,2048]{1,0:T(8,128)(2,1)S(1)} %copy-done.50, ...), custom_call_target="tpu_custom_call" | custom-call | flops 1 | bytes 1 | tf_op jit(solution)/shard_map/cond/branch_1_fun/dh1/pallas_call | solution.py:44
  568.6 23.7 %conditional.16 = (f32[520,1024]{1,0:T(8,128)}, bf16[520,1024]{1,0:T(8,128)(2,1)}, f32[4,1024]{1,0:T(4,128)S(1)}, bf16[520,1024]{1,0:T(8,128)(2,1)}) conditional(s32[]{:T(128)} %bitcast.2, () %tuple.121, (s32[5]{0:T(128)S(1)}, bf16[1040,1024]{1,0:T(8,128)(2,1)S(1)}, bf16[4,128,2048]{2,1,0:T(8,128)(2,1)}, bf16[4,128,2048]{2,1,0:T(8,128)(2,1)}, ...), branch_computations={%region_14.15_spmd, %region_15.16_spmd} | conditional | flops 2 | bytes 8519794 | solution.py:717
  603.9 30.0 %attn_bwd.3 = (bf16[3,1040,512]{2,1,0:T(8,128)(2,1)S(1)}, f32[2,1,512]{2,1,0:T(1,128)S(1)}) custom-call(bf16[1040,1536]{1,0:T(8,128)(2,1)S(1)} %get-tuple-element.395.q_ref.k_ref.v_ref, bf16[1040,1536]{1,0:T(8,128)(2,1)S(1)} %get-tuple-element.395.q_ref.k_ref.v_ref, bf16[1040,1536]{1,0:T(8,128)(2,1)S(1)} %get-tuple-element.395.q_ref.k_ref.v_ref, ...), custom_call_target="tpu_custom_call" | custom-call | flops 1 | bytes 1 | tf_op jit(solution)/shard_map/attn_bwd/pallas_call | solution.py:44
  641.3 44.8 %collective-permute-done.31.rest_0_ = bf16[1024,1024]{1,0:T(8,128)(2,1)S(1)} collective-permute-done((bf16[1024,1024]{1,0:T(8,128)(2,1)}, bf16[1024,1024]{1,0:T(8,128)(2,1)S(1)}, u32[]{:S(2)}, u32[]{:S(2)}) %collective-permute-start.31) | collective-permute-done | bytes 2097184 | tf_op jit(solution)/shard_map/ppermute | solution.py:633
  719.3 26.9 %collective-permute-done.41.recv = bf16[4,128,2048]{2,1,0:T(8,128)(2,1)} collective-permute-done((bf16[4,128,2048]{2,1,0:T(8,128)(2,1)}, bf16[4,128,2048]{2,1,0:T(8,128)(2,1)}, u32[]{:S(2)}, u32[]{:S(2)}) %collective-permute-start.41) | collective-permute-done | bytes 2097184 | tf_op jit(solution)/shard_map/ppermute | solution.py:637
  749.6 14.6 %adam_mlp.2 = (f32[2,128,8192]{2,1,0:T(8,128)}, f32[2,128,8192]{2,1,0:T(8,128)}, f32[2,128,8192]{2,1,0:T(8,128)}, f32[2,128,8192]{2,1,0:T(8,128)}) custom-call(s32[5]{0:T(128)S(1)} %stack.48.ids, bf16[2,128,2048]{2,1,0:T(8,128)(2,1)S(1)} %pad_maximum_fusion.rest_0_, bf16[2,128,2048]{2,1,0:T(8,128)(2,1)S(1)} %collective-permute-done.36.rest_1_, ...), custom_call_target="tpu_custom_call" | custom-call | flops 1 | bytes 1 | tf_op jit(solution)/shard_map/adam_mlp/pallas_call | solution.py:44
  770.1 18.6 %collective-permute-done.32.recv = bf16[4,128,2048]{2,1,0:T(8,128)(2,1)} collective-permute-done((bf16[4,128,2048]{2,1,0:T(8,128)(2,1)}, bf16[4,128,2048]{2,1,0:T(8,128)(2,1)}, u32[]{:S(2)}, u32[]{:S(2)}) %collective-permute-start.32) | collective-permute-done | bytes 2097184 | tf_op jit(solution)/shard_map/ppermute | solution.py:637
  800.2 20.2 %conditional.17 = (f32[2,1024]{1,0:T(2,128)S(1)}, f32[1,520,1024]{2,1,0:T(8,128)}) conditional(s32[]{:T(128)} %bitcast.2, () %tuple.120, (s32[5]{0:T(128)S(1)}, bf16[3,1040,512]{2,1,0:T(8,128)(2,1)}, bf16[1024,2048]{1,0:T(8,128)(2,1)S(1)}, bf16[520,1024]{1,0:T(8,128)(2,1)S(1)}, f32[520,1024]{1,0:T(8,128)}, ...), branch_computations={%region_17.18_spmd, %region_18.19_spmd} | conditional | flops 2 | bytes 17039444 | solution.py:717
  834.3 18.8 %collective-permute-done.38 = bf16[1,128,2048]{2,1,0:T(8,128)(2,1)S(1)} collective-permute-done((bf16[1,128,2048]{2,1,0:T(8,128)(2,1)S(1)}, bf16[1,128,2048]{2,1,0:T(8,128)(2,1)S(1)}, u32[]{:S(2)}, u32[]{:S(2)}) %collective-permute-start.38) | collective-permute-done | bytes 524320 | tf_op jit(solution)/shard_map/ppermute | solution.py:637
  855.6 14.4 %collective-permute-done.47 = f32[2,16,1024]{2,1,0:T(8,128)S(1)} collective-permute-done((f32[2,16,1024]{2,1,0:T(8,128)S(1)}, f32[2,16,1024]{2,1,0:T(8,128)S(1)}, u32[]{:S(2)}, u32[]{:S(2)}) %collective-permute-start.47) | collective-permute-done | bytes 131104 | tf_op jit(solution)/shard_map/ppermute | solution.py:633
  892.4 14.8 %adam_mlp.3 = (f32[2,128,8192]{2,1,0:T(8,128)}, f32[2,128,8192]{2,1,0:T(8,128)}, f32[2,128,8192]{2,1,0:T(8,128)}, f32[2,128,8192]{2,1,0:T(8,128)}) custom-call(s32[5]{0:T(128)S(1)} %stack.48.ids, bf16[2,128,2048]{2,1,0:T(8,128)(2,1)S(1)} %pad_maximum_fusion.1.rest_0_, ...), custom_call_target="tpu_custom_call", output_to_operand_aliasing={{0}: (6, {}), {1}: (7, {}), {2}: (8, {}), {3}: (9, {})} | custom-call | flops 1 | bytes 1 | tf_op jit(solution)/shard_map/adam_mlp/pallas_call | solution.py:44
  (377 shorter events, 496.1 us)
Async XLA Ops:
  7.2 115.0 %all-gather.3.cloned.1.call-start = ((), (), s32[]{:S(2)}) async-start(), calls=%async_computation.2 | async-start | bytes 4718592 | tf_op jit(solution)/shard_map/all_gather | solution.py:787
  11.0 279.3 %all-gather.5.cloned.1.call-start = ((), (), s32[]{:S(2)}) async-start(), calls=%async_computation.3 | async-start | bytes 4718592 | tf_op jit(solution)/shard_map/all_gather | solution.py:787
  34.9 73.9 %collective-permute-start.20 = (bf16[128,2048]{1,0:T(8,128)(2,1)S(1)}, bf16[128,2048]{1,0:T(8,128)(2,1)S(1)}, u32[]{:S(2)}, u32[]{:S(2)}) collective-permute-start(bf16[128,2048]{1,0:T(8,128)(2,1)S(1)} %pick_m.2.rest_0_), channel_id=1, source_target_pairs={{0,8},{2,10},{4,12},{6,14},{8,0},{10,2},{12,4},{14,6},{1,9},{3,11}... | collective-permute-start | bytes 1572872 | tf_op jit(solution)/shard_map/ppermute | solution.py:675
  34.9 73.9 %collective-permute-start.19 = (bf16[128,2048]{1,0:T(8,128)(2,1)S(1)}, bf16[128,2048]{1,0:T(8,128)(2,1)S(1)}, u32[]{:S(2)}, u32[]{:S(2)}) collective-permute-start(bf16[128,2048]{1,0:T(8,128)(2,1)S(1)} %pick_m.2.rest_0_), channel_id=1, source_target_pairs={{0,4},{2,6},{4,8},{6,10},{8,12},{10,14},{12,0},{14,2},{1,5},{3,7},... | collective-permute-start | bytes 1572872 | tf_op jit(solution)/shard_map/ppermute | solution.py:675
  111.5 51.9 %collective-permute-start.23 = (bf16[4,128,2048]{2,1,0:T(8,128)(2,1)}, bf16[4,128,2048]{2,1,0:T(8,128)(2,1)}, u32[]{:S(2)}, u32[]{:S(2)}) collective-permute-start(bf16[4,128,2048]{2,1,0:T(8,128)(2,1)} %merge_z.1.rest_0_), channel_id=1, source_target_pairs={{0,16},{16,0},{1,17},{17,1},{2,18},{18,2},{3,19},{19,3},{4,20},{20... | collective-permute-start | bytes 6291464 | tf_op jit(solution)/shard_map/ppermute | solution.py:633
  112.9 51.2 %collective-permute-start.22 = (bf16[4,128,2048]{2,1,0:T(8,128)(2,1)}, bf16[4,128,2048]{2,1,0:T(8,128)(2,1)}, u32[]{:S(2)}, u32[]{:S(2)}) collective-permute-start(bf16[4,128,2048]{2,1,0:T(8,128)(2,1)} %merge_z.1.rest_0_), channel_id=1, source_target_pairs={{0,2},{2,0},{4,6},{6,4},{8,10},{10,8},{12,14},{14,12},{1,3},{3,1},... | collective-permute-start | bytes 6291464 | tf_op jit(solution)/shard_map/ppermute | solution.py:637
  115.2 477.1 %reduce-scatter.3.cloned.1.call-start = ((), (), s32[]{:S(2)}) async-start(), calls=%async_computation.4 | async-start | bytes 9437184 | tf_op jit(solution)/shard_map/reduce_scatter | solution.py:964
  115.3 48.1 %collective-permute-start.24 = (bf16[1,128,2048]{2,1,0:T(8,128)(2,1)}, bf16[1,128,2048]{2,1,0:T(8,128)(2,1)}, u32[]{:S(2)}, u32[]{:S(2)}) collective-permute-start(bf16[1,128,2048]{2,1,0:T(8,128)(2,1)} %bitcast.13.own), channel_id=1, source_target_pairs={{0,8},{2,10},{4,12},{6,14},{8,0},{10,2},{12,4},{14,6},{1,9},{3,11}... | collective-permute-start | bytes 1572872 | tf_op jit(solution)/shard_map/ppermute | solution.py:637
  166.9 69.7 %collective-permute-start.25 = (bf16[2,128,2048]{2,1,0:T(8,128)(2,1)}, bf16[2,128,2048]{2,1,0:T(8,128)(2,1)}, u32[]{:S(2)}, u32[]{:S(2)}) collective-permute-start(bf16[2,128,2048]{2,1,0:T(8,128)(2,1)} %bitcast.14.own), channel_id=1, source_target_pairs={{0,4},{2,6},{4,0},{6,2},{8,12},{10,14},{12,8},{14,10},{1,5},{3,7},... | collective-permute-start | bytes 3145736 | tf_op jit(solution)/shard_map/ppermute | solution.py:637
  185.4 69.6 %collective-permute-start.26 = (bf16[4,128,2048]{2,1,0:T(8,128)(2,1)}, bf16[4,128,2048]{2,1,0:T(8,128)(2,1)}, u32[]{:S(2)}, u32[]{:S(2)}) collective-permute-start(bf16[4,128,2048]{2,1,0:T(8,128)(2,1)} %collective-permute-done.22.rest_1_), channel_id=1, source_target_pairs={{0,16},{16,0},{1,17},{17,1},{2,18},{18,2},{3,19},{19,3},{4,20},{20... | collective-permute-start | bytes 6291464 | tf_op jit(solution)/shard_map/ppermute | solution.py:633
  241.1 47.7 %collective-permute-start.27 = (bf16[4,128,2048]{2,1,0:T(8,128)(2,1)}, bf16[4,128,2048]{2,1,0:T(8,128)(2,1)}, u32[]{:S(2)}, u32[]{:S(2)}) collective-permute-start(bf16[4,128,2048]{2,1,0:T(8,128)(2,1)} %bitcast.15.rest_0_), channel_id=1, source_target_pairs={{0,2},{2,0},{4,6},{6,4},{8,10},{10,8},{12,14},{14,12},{1,3},{3,1},... | collective-permute-start | bytes 6291464 | tf_op jit(solution)/shard_map/ppermute | solution.py:637
  253.5 48.9 %collective-permute-start.28 = (bf16[4,128,2048]{2,1,0:T(8,128)(2,1)}, bf16[4,128,2048]{2,1,0:T(8,128)(2,1)}, u32[]{:S(2)}, u32[]{:S(2)}) collective-permute-start(bf16[4,128,2048]{2,1,0:T(8,128)(2,1)} %bitcast.15.rest_0_), channel_id=1, source_target_pairs={{0,16},{16,0},{1,17},{17,1},{2,18},{18,2},{3,19},{19,3},{4,20},{20... | collective-permute-start | bytes 6291464 | tf_op jit(solution)/shard_map/ppermute | solution.py:633
  288.8 57.0 %collective-permute-start.29 = (bf16[4,128,2048]{2,1,0:T(8,128)(2,1)}, bf16[4,128,2048]{2,1,0:T(8,128)(2,1)}, u32[]{:S(2)}, u32[]{:S(2)}) collective-permute-start(bf16[4,128,2048]{2,1,0:T(8,128)(2,1)} %collective-permute-done.27.rest_1_), channel_id=1, source_target_pairs={{0,16},{16,0},{1,17},{17,1},{2,18},{18,2},{3,19},{19,3},{4,20},{20... | collective-permute-start | bytes 6291464 | tf_op jit(solution)/shard_map/ppermute | solution.py:633
  443.9 255.5 %reduce-scatter.5.cloned.1.call-start = ((), (), s32[]{:S(2)}) async-start(), calls=%async_computation.5 | async-start | bytes 4718592 | tf_op jit(solution)/shard_map/reduce_scatter | solution.py:985
  592.4 48.9 %collective-permute-start.30 = (bf16[1024,1024]{1,0:T(8,128)(2,1)}, bf16[1024,1024]{1,0:T(8,128)(2,1)S(1)}, u32[]{:S(2)}, u32[]{:S(2)}) collective-permute-start(bf16[1024,1024]{1,0:T(8,128)(2,1)} %copy-done.44), channel_id=1, source_target_pairs={{0,16},{16,0},{1,17},{17,1},{2,18},{18,2},{3,19},{19,3},{4,20},{20... | collective-permute-start | bytes 6291464 | tf_op jit(solution)/shard_map/ppermute | solution.py:633
  594.1 92.0 %collective-permute-start.31 = (bf16[1024,1024]{1,0:T(8,128)(2,1)}, bf16[1024,1024]{1,0:T(8,128)(2,1)S(1)}, u32[]{:S(2)}, u32[]{:S(2)}) collective-permute-start(bf16[1024,1024]{1,0:T(8,128)(2,1)} %copy-done.43), channel_id=1, source_target_pairs={{0,16},{16,0},{1,17},{17,1},{2,18},{18,2},{3,19},{19,3},{4,20},{20... | collective-permute-start | bytes 6291464 | tf_op jit(solution)/shard_map/ppermute | solution.py:633
  594.5 114.2 %collective-permute-start.35 = (bf16[128,4096]{1,0:T(8,128)(2,1)}, bf16[128,4096]{1,0:T(8,128)(2,1)}, u32[]{:S(2)}, u32[]{:S(2)}) collective-permute-start(bf16[128,4096]{1,0:T(8,128)(2,1)} %reduce-scatter.3.cloned.1.call-done), channel_id=1, source_target_pairs={{0,16},{16,0},{1,17},{17,1},{2,18},{18,2},{3,19},{19,3},{4,20},{20... | collective-permute-start | bytes 3145736 | tf_op jit(solution)/shard_map/ppermute | solution.py:633
  697.3 48.9 %collective-permute-start.41 = (bf16[4,128,2048]{2,1,0:T(8,128)(2,1)}, bf16[4,128,2048]{2,1,0:T(8,128)(2,1)}, u32[]{:S(2)}, u32[]{:S(2)}) collective-permute-start(bf16[4,128,2048]{2,1,0:T(8,128)(2,1)} %get-tuple-element.516), channel_id=1, source_target_pairs={{0,2},{2,0},{4,6},{6,4},{8,10},{10,8},{12,14},{14,12},{1,3},{3,1},... | collective-permute-start | bytes 6291464 | tf_op jit(solution)/shard_map/ppermute | solution.py:637
  698.7 90.0 %collective-permute-start.32 = (bf16[4,128,2048]{2,1,0:T(8,128)(2,1)}, bf16[4,128,2048]{2,1,0:T(8,128)(2,1)}, u32[]{:S(2)}, u32[]{:S(2)}) collective-permute-start(bf16[4,128,2048]{2,1,0:T(8,128)(2,1)} %get-tuple-element.492), channel_id=1, source_target_pairs={{0,2},{2,0},{4,6},{6,4},{8,10},{10,8},{12,14},{14,12},{1,3},{3,1},... | collective-permute-start | bytes 6291464 | tf_op jit(solution)/shard_map/ppermute | solution.py:637
  710.7 39.0 %collective-permute-start.36 = (bf16[2,128,2048]{2,1,0:T(8,128)(2,1)S(1)}, bf16[2,128,2048]{2,1,0:T(8,128)(2,1)S(1)}, u32[]{:S(2)}, u32[]{:S(2)}) collective-permute-start(bf16[2,128,2048]{2,1,0:T(8,128)(2,1)S(1)} %pad_maximum_fusion.rest_0_), channel_id=1, source_target_pairs={{0,1},{1,0},{2,3},{3,2},{4,5},{5,4},{6,7},{7,6},{8,9},{9,8},{10,11... | collective-permute-start | bytes 3145736 | tf_op jit(solution)/shard_map/ppermute | solution.py:629
  719.2 45.0 %collective-permute-start.34 = (bf16[128,2048]{1,0:T(8,128)(2,1)S(1)}, bf16[128,2048]{1,0:T(8,128)(2,1)S(1)}, u32[]{:S(2)}, u32[]{:S(2)}) collective-permute-start(bf16[128,2048]{1,0:T(8,128)(2,1)S(1)} %add_convert_fusion.5.rest_0_), channel_id=1, source_target_pairs={{0,1},{1,0},{2,3},{3,2},{4,5},{5,4},{6,7},{7,6},{8,9},{9,8},{10,11... | collective-permute-start | bytes 1572872 | tf_op jit(solution)/shard_map/ppermute | solution.py:629
  749.5 44.0 %collective-permute-start.42 = (bf16[2,128,2048]{2,1,0:T(8,128)(2,1)S(1)}, bf16[2,128,2048]{2,1,0:T(8,128)(2,1)S(1)}, u32[]{:S(2)}, u32[]{:S(2)}) collective-permute-start(bf16[2,128,2048]{2,1,0:T(8,128)(2,1)S(1)} %get-tuple-element.518), channel_id=1, source_target_pairs={{0,4},{2,6},{4,0},{6,2},{8,12},{10,14},{12,8},{14,10},{1,5},{3,7},... | collective-permute-start | bytes 3145736 | tf_op jit(solution)/shard_map/ppermute | solution.py:637
  796.5 34.7 %collective-permute-start.43 = (bf16[1,128,2048]{2,1,0:T(8,128)(2,1)}, bf16[1,128,2048]{2,1,0:T(8,128)(2,1)}, u32[]{:S(2)}, u32[]{:S(2)}) collective-permute-start(bf16[1,128,2048]{2,1,0:T(8,128)(2,1)} %get-tuple-element.520), channel_id=1, source_target_pairs={{0,8},{2,10},{4,12},{6,14},{8,0},{10,2},{12,4},{14,6},{1,9},{3,11}... | collective-permute-start | bytes 1572872 | tf_op jit(solution)/shard_map/ppermute | solution.py:637
  871.1 36.1 %collective-permute-start.40 = (bf16[128,2048]{1,0:T(8,128)(2,1)}, bf16[128,2048]{1,0:T(8,128)(2,1)}, u32[]{:S(2)}, u32[]{:S(2)}) collective-permute-start(bf16[128,2048]{1,0:T(8,128)(2,1)} %add_convert_fusion.1.rest_0_), channel_id=1, source_target_pairs={{0,1},{1,0},{2,3},{3,2},{4,5},{5,4},{6,7},{7,6},{8,9},{9,8},{10,11... | collective-permute-start | bytes 1572872 | tf_op jit(solution)/shard_map/ppermute | solution.py:629
  (122 other events, 1458.9 us)
Sparse Core Ops, SparseCore 0:
  11.1 111.0 all-gather.2
  124.9 109.5 all-gather.4
  444.0 148.2 reduce-scatter.2
  596.8 86.9 reduce-scatter.4

commit v2 on v1

--- a/solution.py
+++ b/solution.py
@@ -815,7 +815,6 @@
             far_a = swap_x(z4)
             pm_next, _ = tie(pm[1][None], z4)
         if staged and l == 1:
-            h_oth, y1 = tie(h_oth, y1)
             z4 = m_four
         qkv, h_t = nn_call(
             ids, h_own, h_oth, wa[l], 0, 3, group, functools.partial(epi_qkv, base=base), [V],
@@ -823,7 +822,8 @@
             "qkv", flip=True,
         )
         if staged and l == 1:
-            qkv, far_a = tie(qkv, far_a)
+            qkv, y1, far_a = tie(qkv, y1, far_a)
+            far_b = swap_x(y1)
         mixed, mixed_wide, lse = attn_fwd(qkv, mb)
         if staged and l == 0:
             m_recv = swap_bit(pm_next, 4)
@@ -832,8 +832,6 @@
             m_two = merge(ids, pm_next, m_recv, IZ1)
             m_recv = swap_bit(m_two, 2)
         if staged and l == 1:
-            far_b = swap_x(y1)
-            mixed, far_b = tie(mixed, far_b)
             wm[1] = [(z4, y1), (far_a, far_b)]
 
         def proj_pair(mixed, w, res, vec):
@@ -854,11 +852,8 @@
         mid, branch, h2_own, h2_oth = apart(go, proj_pair, mixed, wa[l], res, vec)
         act, gp = [], []
         for i in (0, 1):
-            if staged and l == 0 and i == 1:
-                h2_own, m_recv = tie(h2_own, m_recv)
-                m_four = merge(ids, m_two, m_recv, IZ0)
-                y1 = swap_bit(m_four, 1)
-                far_a = swap_x(m_four)
+            if i == 1:
+                h2_own, act[0] = tie(h2_own, act[0])
             got = nn_call(
                 ids, h2_own, h2_oth, wm[l][i], 0, wide // nb, nb,
                 functools.partial(epi_up, base=base, own=i == 0), [V],
@@ -869,6 +864,11 @@
             if i == 0:
                 h2_t = got[2]
 
+        if staged and l == 0:
+            act[0], act[1], m_recv = tie(act[0], act[1], m_recv)
+            m_four = merge(ids, m_two, m_recv, IZ0)
+            y1 = swap_bit(m_four, 1)
+            far_a = swap_x(m_four)
         last = l == layers - 1
 
         def down_pair(act, wm, mid, vec, cot):
@@ -1001,15 +1001,6 @@
             pend[("a", l)] = d_a[0]
         else:
             step_y("a", d_a)
-            d_qkv, *far = tie(d_qkv, *far)
-            near = ()
-            for n, (a_t, b) in enumerate(((h2_t, du[0]), (dd_t, act[0]))):
-                near = dw_call(
-                    ids, a_t, b, colspec, wide, [(far[n], 0)], "dw_near", flat=flat,
-                    total=2 * wide, col=n * wide, old=near,
-                )
-            d_qkv, near = tie(d_qkv, near)
-            step_y("m", near)
         down_below = saved[l - 1][-1] if lower else None
 
         def dh1_pair(d_qkv, w, res, dm, vec, down_below):
@@ -1028,6 +1019,20 @@
             return got, swap_core(got[1]) if lower else ()
 
         got, below_oth = apart(go, dh1_pair, d_qkv, wa[l], res, dm, vec, down_below)
+        if split:
+            g_first, *far = tie(got[0], *far)
+            near = ()
+            for n, (a_t, b) in enumerate(((h2_t, du[0]), (dd_t, act[0]))):
+                near = dw_call(
+                    ids, a_t, b, colspec, wide, [(far[n], 0)], "dw_near", flat=flat,
+                    total=2 * wide, col=n * wide, old=near,
+                )
+            g_first, near = tie(g_first, near)
+            step_y("m", near)
+            if staged:
+                pend["a"], _ = tie(pend["a"], near)
+                step_z0("a")
+            got = [g_first] + list(got[1:])
         sums1 = got[2] if lower else got[1]
 
         (gvecs[l],) = call(
@@ -1043,12 +1048,24 @@
             dd_own, dd_oth, dsums = got[1], below_oth, got[3]
     grad_tokens = g
 
+    gv = jnp.stack(gvecs)
+    if staged:
+        gv, _ = tie(gv, pend["a"])
+        gv = gv + swap_core(gv)
+        gv = gv + swap_x(gv)
+        for bit in (1, 2, 4):
+            gv = gv + swap_bit(gv, bit)
+    else:
+        gv = lax.psum(gv, ("dp", "fsdp", "seq"))
+
     for l in reversed(range(layers)):
         if l == 0 and staged:
-            pend["a"], old_a, old_m = tie(pend["a"], tuple(old_a), tuple(old_m))
-            for step in (step_z0, step_z1):
-                for key in ("a", "m"):
-                    step(key)
+            pend["m"], pend["a"], old_a, old_m = tie(
+                pend["m"], pend["a"], tuple(old_a), tuple(old_m)
+            )
+            step_z0("m")
+            pend["m"], gv = tie(pend["m"], gv)
+            step_z1("m")
             g_a, g_m = step_end("a").astype(bf16), step_end("m").astype(bf16)
         elif l == 0:
             g_a, g_m = pend["a"], pend["m"]
@@ -1056,7 +1073,11 @@
             g_a, g_m = pend[("a", l)], pend[("m", l)]
         g_a = (g_a.astype(f32) + swap_x(g_a).astype(f32)).astype(bf16)
         if l > 0:
-            r_m = swap_x(g_m)
+            late, _ = tie(g_m, far[1])
+            r_m = swap_x(late)
+            if staged:
+                r_m, pend["a"] = tie(r_m, pend["a"])
+                step_z1("a")
             n = 2 * wide
             g_m = jnp.stack(
                 [
@@ -1066,27 +1087,26 @@
             )
         else:
             g_m = jnp.stack([g_m, swap_x(g_m)])
+        if l == 0:
+            g_a_both = tie(g_a, swap_core(g_a))
         g_mt = swap_core(g_m)
-        g_at = swap_core(g_a)
+        if l == 0:
+            g_a, g_at = g_a_both
+        else:
+            g_at = swap_core(g_a)
         aspec = pl.BlockSpec((shard, group), lambda b, ids: (0, b // 2))
         old_a = adam_call(
             ids, l, [g_a, g_at], [aspec, aspec], attn_weights, first_attn, second_attn,
             group, pick_attn, old_a, "adam_attn",
         )
+        if l == 0:
+            g_m, g_mt, old_a = tie(g_m, g_mt, tuple(old_a))
         mspec = pl.BlockSpec((2, shard, wide), lambda b, ids: (0, 0, b // 4))
         old_m = adam_call(
             ids, l, [g_m, g_mt], [mspec] * 2, mlp_weights, first_mlp, second_mlp,
             wide, pick_mlp, old_m, "adam_mlp",
         )
 
-    gv = jnp.stack(gvecs)
-    if staged:
-        gv = gv + swap_core(gv)
-        gv = gv + swap_x(gv)
-        for bit in (1, 2, 4):
-            gv = gv + swap_bit(gv, bit)
-    else:
-        gv = lax.psum(gv, ("dp", "fsdp", "seq"))
     gv = lax.dynamic_slice_in_dim(gv, f * (wide // n_fsdp), wide // n_fsdp, axis=2)
     gv = gv[:, :ROWS]
     step_v, one_v, two_v = adam_math(vectors, gv, first_vec, second_vec, RATE_V, 0.0)

time: 930 us -> 877 us (0.943)
  waiting for transfers between devices: 332 us -> 296 us
  starting transfers between devices: 63.2 us -> 49.6 us
    ppermute x16, waiting for transfers between devices: 128 us -> 70.3 us  [swap_bit(): return lax.ppermute(a, 'fsdp', [(i, i ^ bit) for i in range(8)])]
    ppermute x16, starting transfers between devices: 41.3 us -> 28.8 us  [swap_bit(): return lax.ppermute(a, 'fsdp', [(i, i ^ bit) for i in range(8)])]
    ppermute x11, waiting for transfers between devices: 91.3 us -> 104 us  [swap_x(): return lax.ppermute(a, 'dp', SWAP)]
    unnamed x173 -> x175, local copies, waits for them, and re-layouts: 33.7 us -> 37.4 us
  transfers between devices with their start and end apart: 55 -> 55, of which waited for: 36 -> 40; matrix products, arithmetic and copies ran while one was open for 1% -> 1% of each run, Pallas kernels for 41% -> 44%
where the time goes in v2:
time: 877 us; the launch traced here: 869 us
  Pallas kernels  463 us (53%)
  waiting for transfers between devices  296 us (34%)
  starting transfers between devices  49.6 us (6%)
  local copies, waits for them, and re-layouts  38.6 us (4%)
  between operations  16.3 us (2%)
    pallas_call x65, Pallas kernels, call(): pl.pallas_call(body, out_shape=[sds(sh, dt) for sh, dt, _ in outs], grid_...  463 us
    ppermute x11, waiting for transfers between devices, swap_x(): return lax.ppermute(a, 'dp', SWAP)  104 us
    ppermute x3, waiting for transfers between devices, gather_z(): lax.ppermute(own, 'fsdp', [(i, (i + 2 * k) % 8) for i in range(8)])  73.1 us
    ppermute x16, waiting for transfers between devices, swap_bit(): return lax.ppermute(a, 'fsdp', [(i, i ^ bit) for i in range(8)])  70.3 us
    ppermute x21, waiting for transfers between devices, swap_core(): return lax.ppermute(a, 'seq', SWAP)  46.9 us
    unnamed x175, local copies, waits for them, and re-layouts  37.4 us
    ppermute x16, starting transfers between devices, swap_bit(): return lax.ppermute(a, 'fsdp', [(i, i ^ bit) for i in range(8)])  28.8 us
  transfers between devices with their start and end apart: 55, of which 40 were waited for; matrix products, arithmetic and copies ran while one was open for 1% of the time, Pallas kernels for 44%

profile of v2, /device:TPU:0, one launch (start us, length us, event | category | flops | bytes accessed | tf_op | source)
XLA Modules:
  0.0 868.7 jit_solution(1271610195796692633)
XLA Ops:
  37.0 16.0 %collective-permute-done.21.rest_3_ = bf16[128,2048]{1,0:T(8,128)(2,1)S(1)} collective-permute-done((bf16[128,2048]{1,0:T(8,128)(2,1)S(1)}, bf16[128,2048]{1,0:T(8,128)(2,1)S(1)}, u32[]{:S(2)}, u32[]{:S(2)}) %collective-permute-start.21) | collective-permute-done | bytes 524320 | tf_op jit(solution)/shard_map/ppermute | solution.py:675
  53.0 57.1 %collective-permute-done.20.rest_2_ = bf16[128,2048]{1,0:T(8,128)(2,1)S(1)} collective-permute-done((bf16[128,2048]{1,0:T(8,128)(2,1)S(1)}, bf16[128,2048]{1,0:T(8,128)(2,1)S(1)}, u32[]{:S(2)}, u32[]{:S(2)}) %collective-permute-start.20) | collective-permute-done | bytes 524320 | tf_op jit(solution)/shard_map/ppermute | solution.py:675
  133.0 30.8 %attn_fwd.2 = (bf16[1040,512]{1,0:T(8,128)(2,1)S(1)}, f32[1040,512]{1,0:T(8,128)S(1)}, f32[8,1,1040]{2,1,0:T(1,128)S(1)}) custom-call(bf16[1040,1536]{1,0:T(8,128)(2,1)S(1)} %get-tuple-element.412.q_ref.k_ref.v_ref, bf16[1040,1536]{1,0:T(8,128)(2,1)S(1)} %get-tuple-element.412.q_ref.k_ref.v_ref, bf16[1040,1536]{1,0:T(8,128)(2,1)S(1)} %get-tuple-element.412.q_ref.k_ref.v_ref, ...), custom_call_target="tpu_custom_call" | custom-call | flops 1 | bytes 1 | tf_op jit(solution)/shard_map/attn_fwd/pallas_call | solution.py:44
  179.1 13.3 %conditional.10 = (f32[520,1024]{1,0:T(8,128)}, bf16[520,1024]{1,0:T(8,128)(2,1)}, bf16[520,1024]{1,0:T(8,128)(2,1)}, bf16[520,1024]{1,0:T(8,128)(2,1)}) conditional(s32[]{:T(128)} %bitcast.1, () %tuple.109, (s32[5]{0:T(128)S(1)}, bf16[1040,512]{1,0:T(8,128)(2,1)S(1)}, bf16[1024,2048]{1,0:T(8,128)(2,1)S(1)}, bf16[520,1024]{1,0:T(8,128)(2,1)S(1)}, ...), branch_computations={%region_2.3_spmd, %region_3.4_spmd} | conditional | flops 2 | bytes 8519794 | solution.py:717
  203.4 15.1 %collective-permute-done.25.rest_1_ = bf16[4,128,2048]{2,1,0:T(8,128)(2,1)} collective-permute-done((bf16[4,128,2048]{2,1,0:T(8,128)(2,1)}, bf16[4,128,2048]{2,1,0:T(8,128)(2,1)}, u32[]{:S(2)}, u32[]{:S(2)}) %collective-permute-start.25) | collective-permute-done | bytes 2097184 | tf_op jit(solution)/shard_map/ppermute | solution.py:633
  237.7 22.4 %conditional.11 = (f32[520,1024]{1,0:T(8,128)}, bf16[520,1024]{1,0:T(8,128)(2,1)}, bf16[520,1024]{1,0:T(8,128)(2,1)}, bf16[520,1024]{1,0:T(8,128)(2,1)}) conditional(s32[]{:T(128)} %bitcast.1, () %tuple.108, (s32[5]{0:T(128)S(1)}, bf16[1040,1024]{1,0:T(8,128)(2,1)S(1)}, bf16[4,128,2048]{2,1,0:T(8,128)(2,1)S(1)}, bf16[4,128,2048]{2,1,0:T(8,128)(2,1)}, ...), branch_computations={%region_4.5_spmd, %region_5.6_spmd} | conditional | flops 2 | bytes 8519794 | solution.py:717
  268.8 13.3 %collective-permute-done.28.rest_0_ = bf16[4,128,2048]{2,1,0:T(8,128)(2,1)} collective-permute-done((bf16[4,128,2048]{2,1,0:T(8,128)(2,1)}, bf16[4,128,2048]{2,1,0:T(8,128)(2,1)}, u32[]{:S(2)}, u32[]{:S(2)}) %collective-permute-start.28) | collective-permute-done | bytes 2097184 | tf_op jit(solution)/shard_map/ppermute | solution.py:633
  284.0 30.8 %attn_fwd.3 = (bf16[1040,512]{1,0:T(8,128)(2,1)S(1)}, f32[1040,512]{1,0:T(8,128)S(1)}, f32[8,1,1040]{2,1,0:T(1,128)S(1)}) custom-call(bf16[1040,1536]{1,0:T(8,128)(2,1)S(1)} %get-tuple-element.435.q_ref.k_ref.v_ref, bf16[1040,1536]{1,0:T(8,128)(2,1)S(1)} %get-tuple-element.435.q_ref.k_ref.v_ref, bf16[1040,1536]{1,0:T(8,128)(2,1)S(1)} %get-tuple-element.435.q_ref.k_ref.v_ref, ...), custom_call_target="tpu_custom_call" | custom-call | flops 1 | bytes 1 | tf_op jit(solution)/shard_map/attn_fwd/pallas_call | solution.py:44
  316.5 14.9 %conditional.12 = (f32[520,1024]{1,0:T(8,128)}, bf16[520,1024]{1,0:T(8,128)(2,1)}, bf16[520,1024]{1,0:T(8,128)(2,1)}, bf16[520,1024]{1,0:T(8,128)(2,1)}) conditional(s32[]{:T(128)} %bitcast.1, () %tuple.107, (s32[5]{0:T(128)S(1)}, bf16[1040,512]{1,0:T(8,128)(2,1)S(1)}, bf16[1024,2048]{1,0:T(8,128)(2,1)S(1)}, f32[520,1024]{1,0:T(8,128)}, ...), branch_computations={%region_6.7_spmd, %region_7.8_spmd} | conditional | flops 2 | bytes 8519794 | solution.py:717
  355.2 22.3 %conditional.13 = (bf16[520,1024]{1,0:T(8,128)(2,1)}, f32[2,1024]{1,0:T(2,128)S(1)}, bf16[520,1024]{1,0:T(8,128)(2,1)}, f32[1,520,1024]{2,1,0:T(8,128)}) conditional(s32[]{:T(128)} %bitcast.1, () %tuple.106, (s32[5]{0:T(128)S(1)}, bf16[1040,1024]{1,0:T(8,128)(2,1)S(1)}, bf16[4,128,2048]{2,1,0:T(8,128)(2,1)}, bf16[4,128,2048]{2,1,0:T(8,128)(2,1)}, ...), branch_computations={%region_8.9_spmd, %region_9.10_spmd} | conditional | flops 2 | bytes 8519794 | solution.py:717
  413.9 24.4 %conditional.14 = (f32[520,1024]{1,0:T(8,128)}, bf16[520,1024]{1,0:T(8,128)(2,1)}, f32[4,1024]{1,0:T(4,128)S(1)}, bf16[520,1024]{1,0:T(8,128)(2,1)}) conditional(s32[]{:T(128)} %bitcast.1, () %tuple.127, (s32[5]{0:T(128)S(1)}, bf16[1040,1024]{1,0:T(8,128)(2,1)}, bf16[4,128,2048]{2,1,0:T(8,128)(2,1)}, bf16[4,128,2048]{2,1,0:T(8,128)(2,1)}, ...), branch_computations={%region_10.11_spmd, %region_11.12_spmd} | conditional | flops 2 | bytes 42598652 | solution.py:717
  445.7 29.9 %attn_bwd.2 = (bf16[3,1040,512]{2,1,0:T(8,128)(2,1)S(1)}, f32[2,1,512]{2,1,0:T(1,128)S(1)}) custom-call(bf16[1040,1536]{1,0:T(8,128)(2,1)S(1)} %copy-done.2, bf16[1040,1536]{1,0:T(8,128)(2,1)S(1)} %copy-done.2, bf16[1040,1536]{1,0:T(8,128)(2,1)S(1)} %copy-done.2, bf16[1040,512]{1,0:T(8,128)(2,1)S(1)} %get-tuple-element.462.do_ref, ...), custom_call_target="tpu_custom_call" | custom-call | flops 1 | bytes 1 | tf_op jit(solution)/shard_map/attn_bwd/pallas_call | solution.py:44
  485.7 25.2 %conditional.15 = (f32[520,1024]{1,0:T(8,128)}, bf16[520,1024]{1,0:T(8,128)(2,1)}, f32[2,1024]{1,0:T(2,128)S(1)}, f32[2,1024]{1,0:T(2,128)S(1)}, bf16[520,1024]{1,0:T(8,128)(2,1)}) conditional(s32[]{:T(128)} %bitcast.1, () %tuple.126, (s32[5]{0:T(128)S(1)}, bf16[3,1040,512]{2,1,0:T(8,128)(2,1)}, bf16[1024,2048]{1,0:T(8,128)(2,1)}, ...), branch_computations={%region_12.13_spmd, %region_13.14_spmd} | conditional | flops 2 | bytes 38076592 | solution.py:717
  495.5 12.2 %dh1.5 = (f32[520,1024]{1,0:T(8,128)}, bf16[520,1024]{1,0:T(8,128)(2,1)}, f32[2,1024]{1,0:T(2,128)S(1)}, f32[2,1024]{1,0:T(2,128)S(1)}) custom-call(s32[5]{0:T(128)S(1)} %get-tuple-element.188.ids, bf16[3,1040,512]{2,1,0:T(8,128)(2,1)S(1)} %copy-done.54, bf16[1024,2048]{1,0:T(8,128)(2,1)S(1)} %copy-done.50, ...), custom_call_target="tpu_custom_call" | custom-call | flops 1 | bytes 1 | tf_op jit(solution)/shard_map/cond/branch_1_fun/dh1/pallas_call | solution.py:44
  538.2 23.5 %conditional.16 = (f32[520,1024]{1,0:T(8,128)}, bf16[520,1024]{1,0:T(8,128)(2,1)}, f32[4,1024]{1,0:T(4,128)S(1)}, bf16[520,1024]{1,0:T(8,128)(2,1)}) conditional(s32[]{:T(128)} %bitcast.1, () %tuple.125, (s32[5]{0:T(128)S(1)}, bf16[1040,1024]{1,0:T(8,128)(2,1)S(1)}, bf16[4,128,2048]{2,1,0:T(8,128)(2,1)S(1)}, bf16[4,128,2048]{2,1,0:T(8,128)(2,1)}, ...), branch_computations={%region_14.15_spmd, %region_15.16_spmd} | conditional | flops 2 | bytes 8519794 | solution.py:717
  573.2 30.0 %attn_bwd.3 = (bf16[3,1040,512]{2,1,0:T(8,128)(2,1)S(1)}, f32[2,1,512]{2,1,0:T(1,128)S(1)}) custom-call(bf16[1040,1536]{1,0:T(8,128)(2,1)S(1)} %get-tuple-element.412.q_ref.k_ref.v_ref, bf16[1040,1536]{1,0:T(8,128)(2,1)S(1)} %get-tuple-element.412.q_ref.k_ref.v_ref, bf16[1040,1536]{1,0:T(8,128)(2,1)S(1)} %get-tuple-element.412.q_ref.k_ref.v_ref, ...), custom_call_target="tpu_custom_call" | custom-call | flops 1 | bytes 1 | tf_op jit(solution)/shard_map/attn_bwd/pallas_call | solution.py:44
  613.3 20.2 %conditional.17 = ((f32[520,1024]{1,0:T(8,128)}, f32[2,1024]{1,0:T(2,128)S(1)})) conditional(s32[]{:T(128)} %bitcast.1, () %tuple.124, (s32[5]{0:T(128)S(1)}, bf16[3,1040,512]{2,1,0:T(8,128)(2,1)S(1)}, bf16[1024,2048]{1,0:T(8,128)(2,1)}, bf16[520,1024]{1,0:T(8,128)(2,1)}, f32[520,1024]{1,0:T(8,128)}, /*index=5*/f32[28,1024]{1,0:T(8,128)S(1)}) %tuple.203), branch_computations={%region_17.18_spmd, %region_18.19_spmd} | conditional | flops 2 | bytes 25297000 | solution.py:717
  633.6 22.5 %collective-permute-done.31.rest_0_ = bf16[1024,1024]{1,0:T(8,128)(2,1)} collective-permute-done((bf16[1024,1024]{1,0:T(8,128)(2,1)}, bf16[1024,1024]{1,0:T(8,128)(2,1)}, u32[]{:S(2)}, u32[]{:S(2)}) %collective-permute-start.31) | collective-permute-done | bytes 2097184 | tf_op jit(solution)/shard_map/ppermute | solution.py:633
  676.4 17.6 %collective-permute-done.33 = bf16[128,4096]{1,0:T(8,128)(2,1)S(1)} collective-permute-done((bf16[128,4096]{1,0:T(8,128)(2,1)S(1)}, bf16[128,4096]{1,0:T(8,128)(2,1)S(1)}, u32[]{:S(2)}, u32[]{:S(2)}) %collective-permute-start.33) | collective-permute-done | bytes 1048608 | tf_op jit(solution)/shard_map/ppermute | solution.py:633
  714.8 14.1 %adam_mlp.2 = (f32[2,128,8192]{2,1,0:T(8,128)}, f32[2,128,8192]{2,1,0:T(8,128)}, f32[2,128,8192]{2,1,0:T(8,128)}, f32[2,128,8192]{2,1,0:T(8,128)}) custom-call(s32[5]{0:T(128)S(1)} %stack.48.ids, bf16[2,128,2048]{2,1,0:T(8,128)(2,1)S(1)} %pad_maximum_fusion.rest_0_, bf16[2,128,2048]{2,1,0:T(8,128)(2,1)S(1)} %collective-permute-done.39.rest_1_, ...), custom_call_target="tpu_custom_call" | custom-call | flops 1 | bytes 1 | tf_op jit(solution)/shard_map/adam_mlp/pallas_call | solution.py:44
  757.9 12.2 %collective-permute-done.44 = f32[2,16,1024]{2,1,0:T(8,128)S(1)} collective-permute-done((f32[2,16,1024]{2,1,0:T(8,128)S(1)}, f32[2,16,1024]{2,1,0:T(8,128)S(1)}, u32[]{:S(2)}, u32[]{:S(2)}) %collective-permute-start.44) | collective-permute-done | bytes 131104 | tf_op jit(solution)/shard_map/ppermute | solution.py:637
  779.3 25.4 %collective-permute-done.46 = bf16[1,128,2048]{2,1,0:T(8,128)(2,1)S(1)} collective-permute-done((bf16[1,128,2048]{2,1,0:T(8,128)(2,1)S(1)}, bf16[1,128,2048]{2,1,0:T(8,128)(2,1)S(1)}, u32[]{:S(2)}, u32[]{:S(2)}) %collective-permute-start.46) | collective-permute-done | bytes 524320 | tf_op jit(solution)/shard_map/ppermute | solution.py:637
  807.2 12.6 %collective-permute-done.47 = bf16[128,2048]{1,0:T(8,128)(2,1)S(1)} collective-permute-done((bf16[128,2048]{1,0:T(8,128)(2,1)S(1)}, bf16[128,2048]{1,0:T(8,128)(2,1)S(1)}, u32[]{:S(2)}, u32[]{:S(2)}) %collective-permute-start.47) | collective-permute-done | bytes 524320 | tf_op jit(solution)/shard_map/ppermute | solution.py:633
  848.2 13.5 %adam_mlp.3 = (f32[2,128,8192]{2,1,0:T(8,128)}, f32[2,128,8192]{2,1,0:T(8,128)}, f32[2,128,8192]{2,1,0:T(8,128)}, f32[2,128,8192]{2,1,0:T(8,128)}) custom-call(s32[5]{0:T(128)S(1)} %stack.48.ids, bf16[2,128,2048]{2,1,0:T(8,128)(2,1)S(1)} %pad_maximum_fusion.1.rest_0_, ...), custom_call_target="tpu_custom_call", output_to_operand_aliasing={{0}: (6, {}), {1}: (7, {}), {2}: (8, {}), {3}: (9, {})} | custom-call | flops 1 | bytes 1 | tf_op jit(solution)/shard_map/adam_mlp/pallas_call | solution.py:44
  (382 shorter events, 500.4 us)
Async XLA Ops:
  7.2 116.9 %all-gather.3.cloned.1.call-start = ((), (), s32[]{:S(2)}) async-start(), calls=%async_computation.2 | async-start | bytes 4718592 | tf_op jit(solution)/shard_map/all_gather | solution.py:787
  11.0 249.2 %all-gather.5.cloned.1.call-start = ((), (), s32[]{:S(2)}) async-start(), calls=%async_computation.3 | async-start | bytes 4718592 | tf_op jit(solution)/shard_map/all_gather | solution.py:787
  34.0 76.1 %collective-permute-start.20 = (bf16[128,2048]{1,0:T(8,128)(2,1)S(1)}, bf16[128,2048]{1,0:T(8,128)(2,1)S(1)}, u32[]{:S(2)}, u32[]{:S(2)}) collective-permute-start(bf16[128,2048]{1,0:T(8,128)(2,1)S(1)} %pick_m.2.rest_0_), channel_id=1, source_target_pairs={{0,8},{2,10},{4,12},{6,14},{8,0},{10,2},{12,4},{14,6},{1,9},{3,11}... | collective-permute-start | bytes 1572872 | tf_op jit(solution)/shard_map/ppermute | solution.py:675
  34.0 76.1 %collective-permute-start.19 = (bf16[128,2048]{1,0:T(8,128)(2,1)S(1)}, bf16[128,2048]{1,0:T(8,128)(2,1)S(1)}, u32[]{:S(2)}, u32[]{:S(2)}) collective-permute-start(bf16[128,2048]{1,0:T(8,128)(2,1)S(1)} %pick_m.2.rest_0_), channel_id=1, source_target_pairs={{0,4},{2,6},{4,8},{6,10},{8,12},{10,14},{12,0},{14,2},{1,5},{3,7},... | collective-permute-start | bytes 1572872 | tf_op jit(solution)/shard_map/ppermute | solution.py:675
  112.7 450.5 %reduce-scatter.3.cloned.1.call-start = ((), (), s32[]{:S(2)}) async-start(), calls=%async_computation.4 | async-start | bytes 9437184 | tf_op jit(solution)/shard_map/reduce_scatter | solution.py:964
  116.9 48.4 %collective-permute-start.23 = (bf16[4,128,2048]{2,1,0:T(8,128)(2,1)}, bf16[4,128,2048]{2,1,0:T(8,128)(2,1)}, u32[]{:S(2)}, u32[]{:S(2)}) collective-permute-start(bf16[4,128,2048]{2,1,0:T(8,128)(2,1)} %merge_z.1.rest_0_), channel_id=1, source_target_pairs={{0,16},{16,0},{1,17},{17,1},{2,18},{18,2},{3,19},{19,3},{4,20},{20... | collective-permute-start | bytes 6291464 | tf_op jit(solution)/shard_map/ppermute | solution.py:633
  118.3 53.3 %collective-permute-start.22 = (bf16[4,128,2048]{2,1,0:T(8,128)(2,1)}, bf16[4,128,2048]{2,1,0:T(8,128)(2,1)}, u32[]{:S(2)}, u32[]{:S(2)}) collective-permute-start(bf16[4,128,2048]{2,1,0:T(8,128)(2,1)} %merge_z.1.rest_0_), channel_id=1, source_target_pairs={{0,2},{2,0},{4,6},{6,4},{8,10},{10,8},{12,14},{14,12},{1,3},{3,1},... | collective-permute-start | bytes 6291464 | tf_op jit(solution)/shard_map/ppermute | solution.py:637
  119.8 45.5 %collective-permute-start.24 = (bf16[1,128,2048]{2,1,0:T(8,128)(2,1)}, bf16[1,128,2048]{2,1,0:T(8,128)(2,1)}, u32[]{:S(2)}, u32[]{:S(2)}) collective-permute-start(bf16[1,128,2048]{2,1,0:T(8,128)(2,1)} %bitcast.12.own), channel_id=1, source_target_pairs={{0,8},{2,10},{4,12},{6,14},{8,0},{10,2},{12,4},{14,6},{1,9},{3,11}... | collective-permute-start | bytes 1572872 | tf_op jit(solution)/shard_map/ppermute | solution.py:637
  171.7 46.8 %collective-permute-start.25 = (bf16[4,128,2048]{2,1,0:T(8,128)(2,1)}, bf16[4,128,2048]{2,1,0:T(8,128)(2,1)}, u32[]{:S(2)}, u32[]{:S(2)}) collective-permute-start(bf16[4,128,2048]{2,1,0:T(8,128)(2,1)} %collective-permute-done.22.rest_1_), channel_id=1, source_target_pairs={{0,16},{16,0},{1,17},{17,1},{2,18},{18,2},{3,19},{19,3},{4,20},{20... | collective-permute-start | bytes 6291464 | tf_op jit(solution)/shard_map/ppermute | solution.py:633
  175.0 55.3 %collective-permute-start.26 = (bf16[2,128,2048]{2,1,0:T(8,128)(2,1)}, bf16[2,128,2048]{2,1,0:T(8,128)(2,1)}, u32[]{:S(2)}, u32[]{:S(2)}) collective-permute-start(bf16[2,128,2048]{2,1,0:T(8,128)(2,1)} %bitcast.13.own), channel_id=1, source_target_pairs={{0,4},{2,6},{4,0},{6,2},{8,12},{10,14},{12,8},{14,10},{1,5},{3,7},... | collective-permute-start | bytes 3145736 | tf_op jit(solution)/shard_map/ppermute | solution.py:637
  234.7 47.3 %collective-permute-start.28 = (bf16[4,128,2048]{2,1,0:T(8,128)(2,1)}, bf16[4,128,2048]{2,1,0:T(8,128)(2,1)}, u32[]{:S(2)}, u32[]{:S(2)}) collective-permute-start(bf16[4,128,2048]{2,1,0:T(8,128)(2,1)} %bitcast.14.rest_0_), channel_id=1, source_target_pairs={{0,16},{16,0},{1,17},{17,1},{2,18},{18,2},{3,19},{19,3},{4,20},{20... | collective-permute-start | bytes 6291464 | tf_op jit(solution)/shard_map/ppermute | solution.py:633
  236.2 47.3 %collective-permute-start.27 = (bf16[4,128,2048]{2,1,0:T(8,128)(2,1)}, bf16[4,128,2048]{2,1,0:T(8,128)(2,1)}, u32[]{:S(2)}, u32[]{:S(2)}) collective-permute-start(bf16[4,128,2048]{2,1,0:T(8,128)(2,1)} %bitcast.14.rest_0_), channel_id=1, source_target_pairs={{0,2},{2,0},{4,6},{6,4},{8,10},{10,8},{12,14},{14,12},{1,3},{3,1},... | collective-permute-start | bytes 6291464 | tf_op jit(solution)/shard_map/ppermute | solution.py:637
  283.5 58.9 %collective-permute-start.29 = (bf16[4,128,2048]{2,1,0:T(8,128)(2,1)}, bf16[4,128,2048]{2,1,0:T(8,128)(2,1)}, u32[]{:S(2)}, u32[]{:S(2)}) collective-permute-start(bf16[4,128,2048]{2,1,0:T(8,128)(2,1)} %collective-permute-done.27.rest_1_), channel_id=1, source_target_pairs={{0,16},{16,0},{1,17},{17,1},{2,18},{18,2},{3,19},{19,3},{4,20},{20... | collective-permute-start | bytes 6291464 | tf_op jit(solution)/shard_map/ppermute | solution.py:633
  413.8 285.1 %reduce-scatter.5.cloned.1.call-start = ((), (), s32[]{:S(2)}) async-start(), calls=%async_computation.5 | async-start | bytes 4718592 | tf_op jit(solution)/shard_map/reduce_scatter | solution.py:985
  563.3 70.3 %collective-permute-start.30 = (bf16[1024,1024]{1,0:T(8,128)(2,1)}, bf16[1024,1024]{1,0:T(8,128)(2,1)}, u32[]{:S(2)}, u32[]{:S(2)}) collective-permute-start(bf16[1024,1024]{1,0:T(8,128)(2,1)} %copy-done.46), channel_id=1, source_target_pairs={{0,16},{16,0},{1,17},{17,1},{2,18},{18,2},{3,19},{19,3},{4,20},{20... | collective-permute-start | bytes 6291464 | tf_op jit(solution)/shard_map/ppermute | solution.py:633
  564.8 91.2 %collective-permute-start.31 = (bf16[1024,1024]{1,0:T(8,128)(2,1)}, bf16[1024,1024]{1,0:T(8,128)(2,1)}, u32[]{:S(2)}, u32[]{:S(2)}) collective-permute-start(bf16[1024,1024]{1,0:T(8,128)(2,1)} %copy-done.45), channel_id=1, source_target_pairs={{0,16},{16,0},{1,17},{17,1},{2,18},{18,2},{3,19},{19,3},{4,20},{20... | collective-permute-start | bytes 6291464 | tf_op jit(solution)/shard_map/ppermute | solution.py:633
  611.8 59.6 %collective-permute-start.34 = (bf16[4,128,2048]{2,1,0:T(8,128)(2,1)}, bf16[4,128,2048]{2,1,0:T(8,128)(2,1)}, u32[]{:S(2)}, u32[]{:S(2)}) collective-permute-start(bf16[4,128,2048]{2,1,0:T(8,128)(2,1)} %get-tuple-element.515), channel_id=1, source_target_pairs={{0,2},{2,0},{4,6},{6,4},{8,10},{10,8},{12,14},{14,12},{1,3},{3,1},... | collective-permute-start | bytes 6291464 | tf_op jit(solution)/shard_map/ppermute | solution.py:637
  670.0 24.0 %collective-permute-start.33 = (bf16[128,4096]{1,0:T(8,128)(2,1)S(1)}, bf16[128,4096]{1,0:T(8,128)(2,1)S(1)}, u32[]{:S(2)}, u32[]{:S(2)}) collective-permute-start(bf16[128,4096]{1,0:T(8,128)(2,1)S(1)} %copy-done.85), channel_id=1, source_target_pairs={{0,16},{16,0},{1,17},{17,1},{2,18},{18,2},{3,19},{19,3},{4,20},{20... | collective-permute-start | bytes 3145736 | tf_op jit(solution)/shard_map/ppermute | solution.py:633
  674.8 24.2 %collective-permute-start.35 = (bf16[2,128,2048]{2,1,0:T(8,128)(2,1)S(1)}, bf16[2,128,2048]{2,1,0:T(8,128)(2,1)S(1)}, u32[]{:S(2)}, u32[]{:S(2)}) collective-permute-start(bf16[2,128,2048]{2,1,0:T(8,128)(2,1)S(1)} %get-tuple-element.519), channel_id=1, source_target_pairs={{0,4},{2,6},{4,0},{6,2},{8,12},{10,14},{12,8},{14,10},{1,5},{3,7},... | collective-permute-start | bytes 3145736 | tf_op jit(solution)/shard_map/ppermute | solution.py:637
  675.5 59.3 %collective-permute-start.32 = (bf16[4,128,2048]{2,1,0:T(8,128)(2,1)}, bf16[4,128,2048]{2,1,0:T(8,128)(2,1)}, u32[]{:S(2)}, u32[]{:S(2)}) collective-permute-start(bf16[4,128,2048]{2,1,0:T(8,128)(2,1)} %get-tuple-element.511), channel_id=1, source_target_pairs={{0,2},{2,0},{4,6},{6,4},{8,10},{10,8},{12,14},{14,12},{1,3},{3,1},... | collective-permute-start | bytes 6291464 | tf_op jit(solution)/shard_map/ppermute | solution.py:637
  712.6 26.5 %collective-permute-start.36 = (bf16[1,128,2048]{2,1,0:T(8,128)(2,1)S(1)}, bf16[1,128,2048]{2,1,0:T(8,128)(2,1)S(1)}, u32[]{:S(2)}, u32[]{:S(2)}) collective-permute-start(bf16[1,128,2048]{2,1,0:T(8,128)(2,1)S(1)} %get-tuple-element.523), channel_id=1, source_target_pairs={{0,8},{2,10},{4,12},{6,14},{8,0},{10,2},{12,4},{14,6},{1,9},{3,11}... | collective-permute-start | bytes 1572872 | tf_op jit(solution)/shard_map/ppermute | solution.py:637
  742.4 35.7 %collective-permute-start.40 = (bf16[2,128,2048]{2,1,0:T(8,128)(2,1)S(1)}, bf16[2,128,2048]{2,1,0:T(8,128)(2,1)S(1)}, u32[]{:S(2)}, u32[]{:S(2)}) collective-permute-start(bf16[2,128,2048]{2,1,0:T(8,128)(2,1)S(1)} %get-tuple-element.538), channel_id=1, source_target_pairs={{0,4},{2,6},{4,0},{6,2},{8,12},{10,14},{12,8},{14,10},{1,5},{3,7},... | collective-permute-start | bytes 3145736 | tf_op jit(solution)/shard_map/ppermute | solution.py:637
  779.3 25.5 %collective-permute-start.46 = (bf16[1,128,2048]{2,1,0:T(8,128)(2,1)S(1)}, bf16[1,128,2048]{2,1,0:T(8,128)(2,1)S(1)}, u32[]{:S(2)}, u32[]{:S(2)}) collective-permute-start(bf16[1,128,2048]{2,1,0:T(8,128)(2,1)S(1)} %get-tuple-element.555), channel_id=1, source_target_pairs={{0,8},{2,10},{4,12},{6,14},{8,0},{10,2},{12,4},{14,6},{1,9},{3,11}... | collective-permute-start | bytes 1572872 | tf_op jit(solution)/shard_map/ppermute | solution.py:637
  819.8 28.4 %collective-permute-start.48 = (bf16[2,128,2048]{2,1,0:T(8,128)(2,1)S(1)}, bf16[2,128,2048]{2,1,0:T(8,128)(2,1)}, u32[]{:S(2)}, u32[]{:S(2)}) collective-permute-start(bf16[2,128,2048]{2,1,0:T(8,128)(2,1)S(1)} %pad_maximum_fusion.1.rest_0_), channel_id=1, source_target_pairs={{0,1},{1,0},{2,3},{3,2},{4,5},{5,4},{6,7},{7,6},{8,9},{9,8},{10,11... | collective-permute-start | bytes 3145736 | tf_op jit(solution)/shard_map/ppermute | solution.py:629
  (124 other events, 1210.2 us)
Sparse Core Ops, SparseCore 0:
  11.1 110.8 all-gather.2
  124.7 103.4 all-gather.4
  413.9 149.3 reduce-scatter.2
  567.8 99.0 reduce-scatter.4

commit v3 on v2

--- a/solution.py
+++ b/solution.py
@@ -1064,14 +1064,19 @@
                 pend["m"], pend["a"], tuple(old_a), tuple(old_m)
             )
             step_z0("m")
-            pend["m"], gv = tie(pend["m"], gv)
             step_z1("m")
-            g_a, g_m = step_end("a").astype(bf16), step_end("m").astype(bf16)
+            g_a = step_end("a").astype(bf16)
         elif l == 0:
             g_a, g_m = pend["a"], pend["m"]
         else:
             g_a, g_m = pend[("a", l)], pend[("m", l)]
         g_a = (g_a.astype(f32) + swap_x(g_a).astype(f32)).astype(bf16)
+        g_at = swap_core(g_a)
+        aspec = pl.BlockSpec((shard, group), lambda b, ids: (0, b // 2))
+        old_a = adam_call(
+            ids, l, [g_a, g_at], [aspec, aspec], attn_weights, first_attn, second_attn,
+            group, pick_attn, old_a, "adam_attn",
+        )
         if l > 0:
             late, _ = tie(g_m, far[1])
             r_m = swap_x(late)
@@ -1086,21 +1091,11 @@
                 ]
             )
         else:
+            if staged:
+                pend["m"], old_a, gv = tie(pend["m"], tuple(old_a), gv)
+                g_m = step_end("m").astype(bf16)
             g_m = jnp.stack([g_m, swap_x(g_m)])
-        if l == 0:
-            g_a_both = tie(g_a, swap_core(g_a))
         g_mt = swap_core(g_m)
-        if l == 0:
-            g_a, g_at = g_a_both
-        else:
-            g_at = swap_core(g_a)
-        aspec = pl.BlockSpec((shard, group), lambda b, ids: (0, b // 2))
-        old_a = adam_call(
-            ids, l, [g_a, g_at], [aspec, aspec], attn_weights, first_attn, second_attn,
-            group, pick_attn, old_a, "adam_attn",
-        )
-        if l == 0:
-            g_m, g_mt, old_a = tie(g_m, g_mt, tuple(old_a))
         mspec = pl.BlockSpec((2, shard, wide), lambda b, ids: (0, 0, b // 4))
         old_m = adam_call(
             ids, l, [g_m, g_mt], [mspec] * 2, mlp_weights, first_mlp, second_mlp,

time: 877 us -> 850 us (0.969)
  waiting for transfers between devices: 296 us -> 275 us
    ppermute x16, waiting for transfers between devices: 70.3 us -> 56 us  [swap_bit(): return lax.ppermute(a, 'fsdp', [(i, i ^ bit) for i in range(8)])]
  transfers between devices with their start and end apart: 55 -> 55, of which waited for: 40 -> 39; matrix products, arithmetic and copies ran while one was open for 1% -> 1% of each run, Pallas kernels for 44% -> 46%
where the time goes in v3:
time: 850 us; the launch traced here: 843 us
  Pallas kernels  458 us (54%)
  waiting for transfers between devices  275 us (32%)
  starting transfers between devices  51 us (6%)
  local copies, waits for them, and re-layouts  37.4 us (4%)
  between operations  16.3 us (2%)
    pallas_call x65, Pallas kernels, call(): pl.pallas_call(body, out_shape=[sds(sh, dt) for sh, dt, _ in outs], grid_...  458 us
    ppermute x11, waiting for transfers between devices, swap_x(): return lax.ppermute(a, 'dp', SWAP)  99.4 us
    ppermute x3, waiting for transfers between devices, gather_z(): lax.ppermute(own, 'fsdp', [(i, (i + 2 * k) % 8) for i in range(8)])  73.1 us
    ppermute x16, waiting for transfers between devices, swap_bit(): return lax.ppermute(a, 'fsdp', [(i, i ^ bit) for i in range(8)])  56 us
    ppermute x21, waiting for transfers between devices, swap_core(): return lax.ppermute(a, 'seq', SWAP)  44.8 us
    unnamed x175, local copies, waits for them, and re-layouts  36.2 us
    ppermute x16, starting transfers between devices, swap_bit(): return lax.ppermute(a, 'fsdp', [(i, i ^ bit) for i in range(8)])  30.2 us
  transfers between devices with their start and end apart: 55, of which 39 were waited for; matrix products, arithmetic and copies ran while one was open for 1% of the time, Pallas kernels for 46%

profile of v3, /device:TPU:0, one launch (start us, length us, event | category | flops | bytes accessed | tf_op | source)
XLA Modules:
  0.0 842.7 jit_solution(2647417021586845368)
XLA Ops:
  37.0 16.0 %collective-permute-done.21.rest_3_ = bf16[128,2048]{1,0:T(8,128)(2,1)S(1)} collective-permute-done((bf16[128,2048]{1,0:T(8,128)(2,1)S(1)}, bf16[128,2048]{1,0:T(8,128)(2,1)S(1)}, u32[]{:S(2)}, u32[]{:S(2)}) %collective-permute-start.21) | collective-permute-done | bytes 524320 | tf_op jit(solution)/shard_map/ppermute | solution.py:675
  53.0 57.1 %collective-permute-done.20.rest_2_ = bf16[128,2048]{1,0:T(8,128)(2,1)S(1)} collective-permute-done((bf16[128,2048]{1,0:T(8,128)(2,1)S(1)}, bf16[128,2048]{1,0:T(8,128)(2,1)S(1)}, u32[]{:S(2)}, u32[]{:S(2)}) %collective-permute-start.20) | collective-permute-done | bytes 524320 | tf_op jit(solution)/shard_map/ppermute | solution.py:675
  133.0 30.8 %attn_fwd.2 = (bf16[1040,512]{1,0:T(8,128)(2,1)S(1)}, f32[1040,512]{1,0:T(8,128)S(1)}, f32[8,1,1040]{2,1,0:T(1,128)S(1)}) custom-call(bf16[1040,1536]{1,0:T(8,128)(2,1)S(1)} %get-tuple-element.408.q_ref.k_ref.v_ref, bf16[1040,1536]{1,0:T(8,128)(2,1)S(1)} %get-tuple-element.408.q_ref.k_ref.v_ref, bf16[1040,1536]{1,0:T(8,128)(2,1)S(1)} %get-tuple-element.408.q_ref.k_ref.v_ref, ...), custom_call_target="tpu_custom_call" | custom-call | flops 1 | bytes 1 | tf_op jit(solution)/shard_map/attn_fwd/pallas_call | solution.py:44
  179.1 13.3 %conditional.10 = (f32[520,1024]{1,0:T(8,128)}, bf16[520,1024]{1,0:T(8,128)(2,1)}, bf16[520,1024]{1,0:T(8,128)(2,1)}, bf16[520,1024]{1,0:T(8,128)(2,1)}) conditional(s32[]{:T(128)} %bitcast.1, () %tuple.107, (s32[5]{0:T(128)S(1)}, bf16[1040,512]{1,0:T(8,128)(2,1)S(1)}, bf16[1024,2048]{1,0:T(8,128)(2,1)S(1)}, bf16[520,1024]{1,0:T(8,128)(2,1)S(1)}, ...), branch_computations={%region_2.3_spmd, %region_3.4_spmd} | conditional | flops 2 | bytes 8519794 | solution.py:717
  203.4 15.1 %collective-permute-done.25.rest_1_ = bf16[4,128,2048]{2,1,0:T(8,128)(2,1)} collective-permute-done((bf16[4,128,2048]{2,1,0:T(8,128)(2,1)}, bf16[4,128,2048]{2,1,0:T(8,128)(2,1)}, u32[]{:S(2)}, u32[]{:S(2)}) %collective-permute-start.25) | collective-permute-done | bytes 2097184 | tf_op jit(solution)/shard_map/ppermute | solution.py:633
  237.7 22.4 %conditional.11 = (f32[520,1024]{1,0:T(8,128)}, bf16[520,1024]{1,0:T(8,128)(2,1)}, bf16[520,1024]{1,0:T(8,128)(2,1)}, bf16[520,1024]{1,0:T(8,128)(2,1)}) conditional(s32[]{:T(128)} %bitcast.1, () %tuple.106, (s32[5]{0:T(128)S(1)}, bf16[1040,1024]{1,0:T(8,128)(2,1)S(1)}, bf16[4,128,2048]{2,1,0:T(8,128)(2,1)S(1)}, bf16[4,128,2048]{2,1,0:T(8,128)(2,1)}, ...), branch_computations={%region_4.5_spmd, %region_5.6_spmd} | conditional | flops 2 | bytes 8519794 | solution.py:717
  268.8 13.3 %collective-permute-done.28.rest_0_ = bf16[4,128,2048]{2,1,0:T(8,128)(2,1)} collective-permute-done((bf16[4,128,2048]{2,1,0:T(8,128)(2,1)}, bf16[4,128,2048]{2,1,0:T(8,128)(2,1)}, u32[]{:S(2)}, u32[]{:S(2)}) %collective-permute-start.28) | collective-permute-done | bytes 2097184 | tf_op jit(solution)/shard_map/ppermute | solution.py:633
  284.0 30.8 %attn_fwd.3 = (bf16[1040,512]{1,0:T(8,128)(2,1)S(1)}, f32[1040,512]{1,0:T(8,128)S(1)}, f32[8,1,1040]{2,1,0:T(1,128)S(1)}) custom-call(bf16[1040,1536]{1,0:T(8,128)(2,1)S(1)} %get-tuple-element.431.q_ref.k_ref.v_ref, bf16[1040,1536]{1,0:T(8,128)(2,1)S(1)} %get-tuple-element.431.q_ref.k_ref.v_ref, bf16[1040,1536]{1,0:T(8,128)(2,1)S(1)} %get-tuple-element.431.q_ref.k_ref.v_ref, ...), custom_call_target="tpu_custom_call" | custom-call | flops 1 | bytes 1 | tf_op jit(solution)/shard_map/attn_fwd/pallas_call | solution.py:44
  316.5 14.9 %conditional.12 = (f32[520,1024]{1,0:T(8,128)}, bf16[520,1024]{1,0:T(8,128)(2,1)}, bf16[520,1024]{1,0:T(8,128)(2,1)}, bf16[520,1024]{1,0:T(8,128)(2,1)}) conditional(s32[]{:T(128)} %bitcast.1, () %tuple.105, (s32[5]{0:T(128)S(1)}, bf16[1040,512]{1,0:T(8,128)(2,1)S(1)}, bf16[1024,2048]{1,0:T(8,128)(2,1)S(1)}, f32[520,1024]{1,0:T(8,128)}, ...), branch_computations={%region_6.7_spmd, %region_7.8_spmd} | conditional | flops 2 | bytes 8519794 | solution.py:717
  355.2 22.3 %conditional.13 = (bf16[520,1024]{1,0:T(8,128)(2,1)}, f32[2,1024]{1,0:T(2,128)S(1)}, bf16[520,1024]{1,0:T(8,128)(2,1)}, f32[1,520,1024]{2,1,0:T(8,128)}) conditional(s32[]{:T(128)} %bitcast.1, () %tuple.104, (s32[5]{0:T(128)S(1)}, bf16[1040,1024]{1,0:T(8,128)(2,1)S(1)}, bf16[4,128,2048]{2,1,0:T(8,128)(2,1)}, bf16[4,128,2048]{2,1,0:T(8,128)(2,1)}, ...), branch_computations={%region_8.9_spmd, %region_9.10_spmd} | conditional | flops 2 | bytes 8519794 | solution.py:717
  413.9 24.4 %conditional.14 = (f32[520,1024]{1,0:T(8,128)}, bf16[520,1024]{1,0:T(8,128)(2,1)}, f32[4,1024]{1,0:T(4,128)S(1)}, bf16[520,1024]{1,0:T(8,128)(2,1)}) conditional(s32[]{:T(128)} %bitcast.1, () %tuple.125, (s32[5]{0:T(128)S(1)}, bf16[1040,1024]{1,0:T(8,128)(2,1)}, bf16[4,128,2048]{2,1,0:T(8,128)(2,1)}, bf16[4,128,2048]{2,1,0:T(8,128)(2,1)}, ...), branch_computations={%region_10.11_spmd, %region_11.12_spmd} | conditional | flops 2 | bytes 42598652 | solution.py:717
  424.1 11.0 %dh2.5 = (f32[520,1024]{1,0:T(8,128)}, bf16[520,1024]{1,0:T(8,128)(2,1)}, f32[4,1024]{1,0:T(4,128)S(1)}) custom-call(s32[5]{0:T(128)S(1)} %get-tuple-element.174.ids, bf16[1040,1024]{1,0:T(8,128)(2,1)S(1)} %copy-done.58, bf16[4,128,2048]{2,1,0:T(8,128)(2,1)} %get-tuple-element.176.rest_1_, bf16[4,128,2048]{2,1,0:T(8,128)(2,1)} %get-tuple-element.177.rest_2_, ...), custom_call_target="tpu_custom_call" | custom-call | flops 1 | bytes 1 | tf_op jit(solution)/shard_map/cond/branch_1_fun/dh2/pallas_call | solution.py:44
  445.7 29.9 %attn_bwd.2 = (bf16[3,1040,512]{2,1,0:T(8,128)(2,1)S(1)}, f32[2,1,512]{2,1,0:T(1,128)S(1)}) custom-call(bf16[1040,1536]{1,0:T(8,128)(2,1)S(1)} %copy-done.2, bf16[1040,1536]{1,0:T(8,128)(2,1)S(1)} %copy-done.2, bf16[1040,1536]{1,0:T(8,128)(2,1)S(1)} %copy-done.2, bf16[1040,512]{1,0:T(8,128)(2,1)S(1)} %get-tuple-element.458.do_ref, ...), custom_call_target="tpu_custom_call" | custom-call | flops 1 | bytes 1 | tf_op jit(solution)/shard_map/attn_bwd/pallas_call | solution.py:44
  485.7 25.2 %conditional.15 = (f32[520,1024]{1,0:T(8,128)}, bf16[520,1024]{1,0:T(8,128)(2,1)}, f32[2,1024]{1,0:T(2,128)S(1)}, f32[2,1024]{1,0:T(2,128)S(1)}, bf16[520,1024]{1,0:T(8,128)(2,1)}) conditional(s32[]{:T(128)} %bitcast.1, () %tuple.124, (s32[5]{0:T(128)S(1)}, bf16[3,1040,512]{2,1,0:T(8,128)(2,1)}, bf16[1024,2048]{1,0:T(8,128)(2,1)}, ...), branch_computations={%region_12.13_spmd, %region_13.14_spmd} | conditional | flops 2 | bytes 38076592 | solution.py:717
  495.5 12.2 %dh1.5 = (f32[520,1024]{1,0:T(8,128)}, bf16[520,1024]{1,0:T(8,128)(2,1)}, f32[2,1024]{1,0:T(2,128)S(1)}, f32[2,1024]{1,0:T(2,128)S(1)}) custom-call(s32[5]{0:T(128)S(1)} %get-tuple-element.188.ids, bf16[3,1040,512]{2,1,0:T(8,128)(2,1)S(1)} %copy-done.54, bf16[1024,2048]{1,0:T(8,128)(2,1)S(1)} %copy-done.50, ...), custom_call_target="tpu_custom_call" | custom-call | flops 1 | bytes 1 | tf_op jit(solution)/shard_map/cond/branch_1_fun/dh1/pallas_call | solution.py:44
  538.2 23.5 %conditional.16 = (f32[520,1024]{1,0:T(8,128)}, bf16[520,1024]{1,0:T(8,128)(2,1)}, f32[4,1024]{1,0:T(4,128)S(1)}, bf16[520,1024]{1,0:T(8,128)(2,1)}) conditional(s32[]{:T(128)} %bitcast.1, () %tuple.123, (s32[5]{0:T(128)S(1)}, bf16[1040,1024]{1,0:T(8,128)(2,1)S(1)}, bf16[4,128,2048]{2,1,0:T(8,128)(2,1)S(1)}, bf16[4,128,2048]{2,1,0:T(8,128)(2,1)}, ...), branch_computations={%region_14.15_spmd, %region_15.16_spmd} | conditional | flops 2 | bytes 8519794 | solution.py:717
  573.2 30.0 %attn_bwd.3 = (bf16[3,1040,512]{2,1,0:T(8,128)(2,1)S(1)}, f32[2,1,512]{2,1,0:T(1,128)S(1)}) custom-call(bf16[1040,1536]{1,0:T(8,128)(2,1)S(1)} %get-tuple-element.408.q_ref.k_ref.v_ref, bf16[1040,1536]{1,0:T(8,128)(2,1)S(1)} %get-tuple-element.408.q_ref.k_ref.v_ref, bf16[1040,1536]{1,0:T(8,128)(2,1)S(1)} %get-tuple-element.408.q_ref.k_ref.v_ref, ...), custom_call_target="tpu_custom_call" | custom-call | flops 1 | bytes 1 | tf_op jit(solution)/shard_map/attn_bwd/pallas_call | solution.py:44
  613.3 20.2 %conditional.17 = ((f32[520,1024]{1,0:T(8,128)}, f32[2,1024]{1,0:T(2,128)S(1)})) conditional(s32[]{:T(128)} %bitcast.1, () %tuple.122, (s32[5]{0:T(128)S(1)}, bf16[3,1040,512]{2,1,0:T(8,128)(2,1)S(1)}, bf16[1024,2048]{1,0:T(8,128)(2,1)}, bf16[520,1024]{1,0:T(8,128)(2,1)}, f32[520,1024]{1,0:T(8,128)}, /*index=5*/f32[28,1024]{1,0:T(8,128)S(1)}) %tuple.199), branch_computations={%region_17.18_spmd, %region_18.19_spmd} | conditional | flops 2 | bytes 25297000 | solution.py:717
  633.6 22.5 %collective-permute-done.31.rest_0_ = bf16[1024,1024]{1,0:T(8,128)(2,1)} collective-permute-done((bf16[1024,1024]{1,0:T(8,128)(2,1)}, bf16[1024,1024]{1,0:T(8,128)(2,1)}, u32[]{:S(2)}, u32[]{:S(2)}) %collective-permute-start.31) | collective-permute-done | bytes 2097184 | tf_op jit(solution)/shard_map/ppermute | solution.py:633
  676.3 17.6 %collective-permute-done.33 = bf16[128,4096]{1,0:T(8,128)(2,1)S(1)} collective-permute-done((bf16[128,4096]{1,0:T(8,128)(2,1)S(1)}, bf16[128,4096]{1,0:T(8,128)(2,1)S(1)}, u32[]{:S(2)}, u32[]{:S(2)}) %collective-permute-start.33) | collective-permute-done | bytes 1048608 | tf_op jit(solution)/shard_map/ppermute | solution.py:633
  715.7 14.1 %adam_mlp.2 = (f32[2,128,8192]{2,1,0:T(8,128)}, f32[2,128,8192]{2,1,0:T(8,128)}, f32[2,128,8192]{2,1,0:T(8,128)}, f32[2,128,8192]{2,1,0:T(8,128)}) custom-call(s32[5]{0:T(128)S(1)} %stack.48.ids, bf16[2,128,2048]{2,1,0:T(8,128)(2,1)S(1)} %pad_maximum_fusion.rest_0_, bf16[2,128,2048]{2,1,0:T(8,128)(2,1)S(1)} %collective-permute-done.39.rest_1_, ...), custom_call_target="tpu_custom_call" | custom-call | flops 1 | bytes 1 | tf_op jit(solution)/shard_map/adam_mlp/pallas_call | solution.py:44
  784.8 13.2 %collective-permute-done.48 = f32[2,16,1024]{2,1,0:T(8,128)S(1)} collective-permute-done((f32[2,16,1024]{2,1,0:T(8,128)S(1)}, f32[2,16,1024]{2,1,0:T(8,128)S(1)}, u32[]{:S(2)}, u32[]{:S(2)}) %collective-permute-start.48) | collective-permute-done | bytes 131104 | tf_op jit(solution)/shard_map/ppermute | solution.py:637
  805.8 12.1 %collective-permute-done.49 = bf16[128,2048]{1,0:T(8,128)(2,1)S(1)} collective-permute-done((bf16[128,2048]{1,0:T(8,128)(2,1)S(1)}, bf16[128,2048]{1,0:T(8,128)(2,1)S(1)}, u32[]{:S(2)}, u32[]{:S(2)}) %collective-permute-start.49) | collective-permute-done | bytes 524320 | tf_op jit(solution)/shard_map/ppermute | solution.py:633
  822.9 12.8 %adam_mlp.3 = (f32[2,128,8192]{2,1,0:T(8,128)}, f32[2,128,8192]{2,1,0:T(8,128)}, f32[2,128,8192]{2,1,0:T(8,128)}, f32[2,128,8192]{2,1,0:T(8,128)}) custom-call(s32[5]{0:T(128)S(1)} %stack.48.ids, bf16[2,128,2048]{2,1,0:T(8,128)(2,1)S(1)} %pad_maximum_fusion.1.rest_0_, ...), custom_call_target="tpu_custom_call", output_to_operand_aliasing={{0}: (6, {}), {1}: (7, {}), {2}: (8, {}), {3}: (9, {})} | custom-call | flops 1 | bytes 1 | tf_op jit(solution)/shard_map/adam_mlp/pallas_call | solution.py:44
  (382 shorter events, 489.0 us)
Async XLA Ops:
  7.2 116.9 %all-gather.3.cloned.1.call-start = ((), (), s32[]{:S(2)}) async-start(), calls=%async_computation.2 | async-start | bytes 4718592 | tf_op jit(solution)/shard_map/all_gather | solution.py:787
  11.0 249.2 %all-gather.5.cloned.1.call-start = ((), (), s32[]{:S(2)}) async-start(), calls=%async_computation.3 | async-start | bytes 4718592 | tf_op jit(solution)/shard_map/all_gather | solution.py:787
  34.0 76.1 %collective-permute-start.20 = (bf16[128,2048]{1,0:T(8,128)(2,1)S(1)}, bf16[128,2048]{1,0:T(8,128)(2,1)S(1)}, u32[]{:S(2)}, u32[]{:S(2)}) collective-permute-start(bf16[128,2048]{1,0:T(8,128)(2,1)S(1)} %pick_m.2.rest_0_), channel_id=1, source_target_pairs={{0,8},{2,10},{4,12},{6,14},{8,0},{10,2},{12,4},{14,6},{1,9},{3,11}... | collective-permute-start | bytes 1572872 | tf_op jit(solution)/shard_map/ppermute | solution.py:675
  34.0 76.1 %collective-permute-start.19 = (bf16[128,2048]{1,0:T(8,128)(2,1)S(1)}, bf16[128,2048]{1,0:T(8,128)(2,1)S(1)}, u32[]{:S(2)}, u32[]{:S(2)}) collective-permute-start(bf16[128,2048]{1,0:T(8,128)(2,1)S(1)} %pick_m.2.rest_0_), channel_id=1, source_target_pairs={{0,4},{2,6},{4,8},{6,10},{8,12},{10,14},{12,0},{14,2},{1,5},{3,7},... | collective-permute-start | bytes 1572872 | tf_op jit(solution)/shard_map/ppermute | solution.py:675
  112.7 450.5 %reduce-scatter.3.cloned.1.call-start = ((), (), s32[]{:S(2)}) async-start(), calls=%async_computation.4 | async-start | bytes 9437184 | tf_op jit(solution)/shard_map/reduce_scatter | solution.py:964
  116.9 48.4 %collective-permute-start.23 = (bf16[4,128,2048]{2,1,0:T(8,128)(2,1)}, bf16[4,128,2048]{2,1,0:T(8,128)(2,1)}, u32[]{:S(2)}, u32[]{:S(2)}) collective-permute-start(bf16[4,128,2048]{2,1,0:T(8,128)(2,1)} %merge_z.1.rest_0_), channel_id=1, source_target_pairs={{0,16},{16,0},{1,17},{17,1},{2,18},{18,2},{3,19},{19,3},{4,20},{20... | collective-permute-start | bytes 6291464 | tf_op jit(solution)/shard_map/ppermute | solution.py:633
  118.3 53.3 %collective-permute-start.22 = (bf16[4,128,2048]{2,1,0:T(8,128)(2,1)}, bf16[4,128,2048]{2,1,0:T(8,128)(2,1)}, u32[]{:S(2)}, u32[]{:S(2)}) collective-permute-start(bf16[4,128,2048]{2,1,0:T(8,128)(2,1)} %merge_z.1.rest_0_), channel_id=1, source_target_pairs={{0,2},{2,0},{4,6},{6,4},{8,10},{10,8},{12,14},{14,12},{1,3},{3,1},... | collective-permute-start | bytes 6291464 | tf_op jit(solution)/shard_map/ppermute | solution.py:637
  119.8 45.5 %collective-permute-start.24 = (bf16[1,128,2048]{2,1,0:T(8,128)(2,1)}, bf16[1,128,2048]{2,1,0:T(8,128)(2,1)}, u32[]{:S(2)}, u32[]{:S(2)}) collective-permute-start(bf16[1,128,2048]{2,1,0:T(8,128)(2,1)} %bitcast.12.own), channel_id=1, source_target_pairs={{0,8},{2,10},{4,12},{6,14},{8,0},{10,2},{12,4},{14,6},{1,9},{3,11}... | collective-permute-start | bytes 1572872 | tf_op jit(solution)/shard_map/ppermute | solution.py:637
  171.7 46.8 %collective-permute-start.25 = (bf16[4,128,2048]{2,1,0:T(8,128)(2,1)}, bf16[4,128,2048]{2,1,0:T(8,128)(2,1)}, u32[]{:S(2)}, u32[]{:S(2)}) collective-permute-start(bf16[4,128,2048]{2,1,0:T(8,128)(2,1)} %collective-permute-done.22.rest_1_), channel_id=1, source_target_pairs={{0,16},{16,0},{1,17},{17,1},{2,18},{18,2},{3,19},{19,3},{4,20},{20... | collective-permute-start | bytes 6291464 | tf_op jit(solution)/shard_map/ppermute | solution.py:633
  175.0 55.3 %collective-permute-start.26 = (bf16[2,128,2048]{2,1,0:T(8,128)(2,1)}, bf16[2,128,2048]{2,1,0:T(8,128)(2,1)}, u32[]{:S(2)}, u32[]{:S(2)}) collective-permute-start(bf16[2,128,2048]{2,1,0:T(8,128)(2,1)} %bitcast.13.own), channel_id=1, source_target_pairs={{0,4},{2,6},{4,0},{6,2},{8,12},{10,14},{12,8},{14,10},{1,5},{3,7},... | collective-permute-start | bytes 3145736 | tf_op jit(solution)/shard_map/ppermute | solution.py:637
  234.7 47.3 %collective-permute-start.28 = (bf16[4,128,2048]{2,1,0:T(8,128)(2,1)}, bf16[4,128,2048]{2,1,0:T(8,128)(2,1)}, u32[]{:S(2)}, u32[]{:S(2)}) collective-permute-start(bf16[4,128,2048]{2,1,0:T(8,128)(2,1)} %bitcast.14.rest_0_), channel_id=1, source_target_pairs={{0,16},{16,0},{1,17},{17,1},{2,18},{18,2},{3,19},{19,3},{4,20},{20... | collective-permute-start | bytes 6291464 | tf_op jit(solution)/shard_map/ppermute | solution.py:633
  236.2 47.3 %collective-permute-start.27 = (bf16[4,128,2048]{2,1,0:T(8,128)(2,1)}, bf16[4,128,2048]{2,1,0:T(8,128)(2,1)}, u32[]{:S(2)}, u32[]{:S(2)}) collective-permute-start(bf16[4,128,2048]{2,1,0:T(8,128)(2,1)} %bitcast.14.rest_0_), channel_id=1, source_target_pairs={{0,2},{2,0},{4,6},{6,4},{8,10},{10,8},{12,14},{14,12},{1,3},{3,1},... | collective-permute-start | bytes 6291464 | tf_op jit(solution)/shard_map/ppermute | solution.py:637
  283.5 58.9 %collective-permute-start.29 = (bf16[4,128,2048]{2,1,0:T(8,128)(2,1)}, bf16[4,128,2048]{2,1,0:T(8,128)(2,1)}, u32[]{:S(2)}, u32[]{:S(2)}) collective-permute-start(bf16[4,128,2048]{2,1,0:T(8,128)(2,1)} %collective-permute-done.27.rest_1_), channel_id=1, source_target_pairs={{0,16},{16,0},{1,17},{17,1},{2,18},{18,2},{3,19},{19,3},{4,20},{20... | collective-permute-start | bytes 6291464 | tf_op jit(solution)/shard_map/ppermute | solution.py:633
  413.8 286.1 %reduce-scatter.5.cloned.1.call-start = ((), (), s32[]{:S(2)}) async-start(), calls=%async_computation.5 | async-start | bytes 4718592 | tf_op jit(solution)/shard_map/reduce_scatter | solution.py:985
  563.3 70.2 %collective-permute-start.30 = (bf16[1024,1024]{1,0:T(8,128)(2,1)}, bf16[1024,1024]{1,0:T(8,128)(2,1)}, u32[]{:S(2)}, u32[]{:S(2)}) collective-permute-start(bf16[1024,1024]{1,0:T(8,128)(2,1)} %copy-done.44), channel_id=1, source_target_pairs={{0,16},{16,0},{1,17},{17,1},{2,18},{18,2},{3,19},{19,3},{4,20},{20... | collective-permute-start | bytes 6291464 | tf_op jit(solution)/shard_map/ppermute | solution.py:633
  564.8 91.2 %collective-permute-start.31 = (bf16[1024,1024]{1,0:T(8,128)(2,1)}, bf16[1024,1024]{1,0:T(8,128)(2,1)}, u32[]{:S(2)}, u32[]{:S(2)}) collective-permute-start(bf16[1024,1024]{1,0:T(8,128)(2,1)} %copy-done.43), channel_id=1, source_target_pairs={{0,16},{16,0},{1,17},{17,1},{2,18},{18,2},{3,19},{19,3},{4,20},{20... | collective-permute-start | bytes 6291464 | tf_op jit(solution)/shard_map/ppermute | solution.py:633
  611.8 59.6 %collective-permute-start.34 = (bf16[4,128,2048]{2,1,0:T(8,128)(2,1)}, bf16[4,128,2048]{2,1,0:T(8,128)(2,1)}, u32[]{:S(2)}, u32[]{:S(2)}) collective-permute-start(bf16[4,128,2048]{2,1,0:T(8,128)(2,1)} %get-tuple-element.511), channel_id=1, source_target_pairs={{0,2},{2,0},{4,6},{6,4},{8,10},{10,8},{12,14},{14,12},{1,3},{3,1},... | collective-permute-start | bytes 6291464 | tf_op jit(solution)/shard_map/ppermute | solution.py:637
  670.0 24.0 %collective-permute-start.33 = (bf16[128,4096]{1,0:T(8,128)(2,1)S(1)}, bf16[128,4096]{1,0:T(8,128)(2,1)S(1)}, u32[]{:S(2)}, u32[]{:S(2)}) collective-permute-start(bf16[128,4096]{1,0:T(8,128)(2,1)S(1)} %copy-done.85), channel_id=1, source_target_pairs={{0,16},{16,0},{1,17},{17,1},{2,18},{18,2},{3,19},{19,3},{4,20},{20... | collective-permute-start | bytes 3145736 | tf_op jit(solution)/shard_map/ppermute | solution.py:633
  674.7 24.2 %collective-permute-start.35 = (bf16[2,128,2048]{2,1,0:T(8,128)(2,1)S(1)}, bf16[2,128,2048]{2,1,0:T(8,128)(2,1)S(1)}, u32[]{:S(2)}, u32[]{:S(2)}) collective-permute-start(bf16[2,128,2048]{2,1,0:T(8,128)(2,1)S(1)} %get-tuple-element.515), channel_id=1, source_target_pairs={{0,4},{2,6},{4,0},{6,2},{8,12},{10,14},{12,8},{14,10},{1,5},{3,7},... | collective-permute-start | bytes 3145736 | tf_op jit(solution)/shard_map/ppermute | solution.py:637
  675.6 60.2 %collective-permute-start.32 = (bf16[4,128,2048]{2,1,0:T(8,128)(2,1)}, bf16[4,128,2048]{2,1,0:T(8,128)(2,1)S(1)}, u32[]{:S(2)}, u32[]{:S(2)}) collective-permute-start(bf16[4,128,2048]{2,1,0:T(8,128)(2,1)} %get-tuple-element.507), channel_id=1, source_target_pairs={{0,2},{2,0},{4,6},{6,4},{8,10},{10,8},{12,14},{14,12},{1,3},{3,1},... | collective-permute-start | bytes 6291464 | tf_op jit(solution)/shard_map/ppermute | solution.py:637
  713.5 26.5 %collective-permute-start.36 = (bf16[1,128,2048]{2,1,0:T(8,128)(2,1)S(1)}, bf16[1,128,2048]{2,1,0:T(8,128)(2,1)S(1)}, u32[]{:S(2)}, u32[]{:S(2)}) collective-permute-start(bf16[1,128,2048]{2,1,0:T(8,128)(2,1)S(1)} %get-tuple-element.519), channel_id=1, source_target_pairs={{0,8},{2,10},{4,12},{6,14},{8,0},{10,2},{12,4},{14,6},{1,9},{3,11}... | collective-permute-start | bytes 1572872 | tf_op jit(solution)/shard_map/ppermute | solution.py:637
  741.6 24.8 %collective-permute-start.40 = (bf16[2,128,2048]{2,1,0:T(8,128)(2,1)S(1)}, bf16[2,128,2048]{2,1,0:T(8,128)(2,1)S(1)}, u32[]{:S(2)}, u32[]{:S(2)}) collective-permute-start(bf16[2,128,2048]{2,1,0:T(8,128)(2,1)S(1)} %get-tuple-element.534), channel_id=1, source_target_pairs={{0,4},{2,6},{4,0},{6,2},{8,12},{10,14},{12,8},{14,10},{1,5},{3,7},... | collective-permute-start | bytes 3145736 | tf_op jit(solution)/shard_map/ppermute | solution.py:637
  756.8 41.2 %collective-permute-start.43 = (bf16[128,2048]{1,0:T(8,128)(2,1)S(1)}, bf16[128,2048]{1,0:T(8,128)(2,1)S(1)}, u32[]{:S(2)}, u32[]{:S(2)}) collective-permute-start(bf16[128,2048]{1,0:T(8,128)(2,1)S(1)} %add_convert_fusion.1.rest_0_), channel_id=1, source_target_pairs={{0,1},{1,0},{2,3},{3,2},{4,5},{5,4},{6,7},{7,6},{8,9},{9,8},{10,11... | collective-permute-start | bytes 1572872 | tf_op jit(solution)/shard_map/ppermute | solution.py:629
  767.5 36.4 %collective-permute-start.41 = (bf16[1,128,2048]{2,1,0:T(8,128)(2,1)S(1)}, bf16[1,128,2048]{2,1,0:T(8,128)(2,1)S(1)}, u32[]{:S(2)}, u32[]{:S(2)}) collective-permute-start(bf16[1,128,2048]{2,1,0:T(8,128)(2,1)S(1)} %get-tuple-element.536), channel_id=1, source_target_pairs={{0,8},{2,10},{4,12},{6,14},{8,0},{10,2},{12,4},{14,6},{1,9},{3,11}... | collective-permute-start | bytes 1572872 | tf_op jit(solution)/shard_map/ppermute | solution.py:637
  (124 other events, 1235.3 us)
Sparse Core Ops, SparseCore 0:
  11.1 110.8 all-gather.2
  124.7 103.4 all-gather.4
  413.9 149.3 reduce-scatter.2
  567.8 99.0 reduce-scatter.4
